TPU v7x, 128 devices: a whole 4x4x4 slice. The times are simulated.
128 devices in a mesh: lat: 8 (over x, core), lon: 16 (over y, z).
Axes of the slice: x: 4, y: 4, z: 4, core: 2. Of those that a mesh axis runs over, the one named last changes fastest.
Arguments:
- tracers: float32 [1024, 1152, 256], P(('lat', 'lon')), may hold values from 0.1 to 3
- phys_fine: bfloat16 [384, 6144, 144], P('lat', 'lon'), may hold values from -2 to 30, as said below
- mix_coarse: bfloat16 [128, 2048, 48], P('lat', 'lon'), may hold values from 0.0049743652 to 0.19921875
- surf_light: float32 [384, 6144], P('lat', 'lon'), may hold values from 0.5 to 4
- land_mask: int32 [128, 2048], P('lat', 'lon'), may hold values from 0 to 1, as said below
- owner_map: int32 [8, 128], P('lat'), may hold values from -1 to 1023, as said below
Outputs:
- tracers_out: float32 [1024, 1152, 256], P(('lat', 'lon'))
- heating: bfloat16 [48, 384, 6144], P(None, 'lat', 'lon')
Inputs may be any that keep to these rules, and one draw needn't show every extreme that they name: `owner_map`: -1 marks a block whose columns are all land, any other value is the slot that holds the block. Slots are numbered band by band, 128 to a band, owner by owner within a band with 8 slots each, and a block's slot lies in its own band. Every band has a multiple of 16 wet blocks. The wet blocks of a band, taken in order of longitude, are held by the owners in turn: the next wet block after one held by owner o is held by owner o + 1 (after 16 - 1 comes 0), also from the band's last wet block to its first; the r-th wet block of a band (from 0) lies in slot r // 16 of its owner. In some band every slot holds a block. `land_mask`: 1 for an ocean column, 0 for land; every column of a block that owner_map marks -1 is land. `phys_fine`: channel c * 48 + l holds level l of: c = 0 the eastward velocity on a fine cell's east face and c = 1 the northward velocity on its north face, as fractions of a cell per step within -0.15 to 0.15; c = 2 temperature within -2 to 30.
All inputs are finite; a program needn't handle non-finite values.
Results may differ from a plain program's by a relative error of at most 0.001.
Values sent between devices are 32-bit elements; how exact they have to be, the bound alone decides.
A program may use at most 192 MiB of HBM per device.

v0:
```python
import jax
import jax.numpy as jnp
from jax import lax
from jax.sharding import PartitionSpec as P

ITERS = 2


diffuse_rate = 0.08
nano_chl_index = 10
diat_chl_index = 11


def extended(cells, sides, width, closed):
    for axis, dim in sides:
        count = lax.axis_size(axis)
        ends = count if closed else count - 1
        head = lax.slice_in_dim(cells, 0, width, axis=dim)
        tail = lax.slice_in_dim(cells, cells.shape[dim] - width, cells.shape[dim], axis=dim)
        cells = jnp.concatenate(
            [
                lax.ppermute(tail, axis, [(i, (i + 1) % count) for i in range(ends)]),
                cells,
                lax.ppermute(head, axis, [((i + 1) % count, i) for i in range(ends)]),
            ],
            axis=dim,
        )
    return cells


def side_by_side(arrays, axis, split_dim, concat_dim, along):
    both = jnp.concatenate(arrays, axis=along)
    filled, at, gathered = (
        lax.all_to_all(both, axis, split_axis=split_dim, concat_axis=concat_dim, tiled=True),
        0,
        [],
    )
    for a in arrays:
        gathered.append(lax.slice_in_dim(filled, at, at + a.shape[along], axis=along))
        at += a.shape[along]
    return tuple(gathered)


def passed_along(x, axis, by):
    size = lax.axis_size(axis)
    return lax.ppermute(x, axis, [(i, (i + by) % size) for i in range(size)])


def positive(value):
    return jnp.maximum(value, 0.0)


def lower_table(levels):
    level_ids = jnp.arange(levels)
    return (level_ids[None, :] < level_ids[:, None]).astype(jnp.float32)


def level_sums(absorb, levels):
    flat_cols = absorb.reshape(levels, -1)
    summed = jnp.dot(
        lower_table(levels),
        flat_cols,
        precision=lax.Precision.HIGHEST,
        preferred_element_type=jnp.float32,
    )
    return summed.reshape(absorb.shape)


def coarsen(fine_band, light_fine, levels, factor):
    row_count = fine_band.shape[0] // factor
    col_count = fine_band.shape[1] // factor
    fine_grid = fine_band.reshape(row_count, factor, col_count, factor, 3, levels)
    east_face = jnp.mean(fine_grid[:, :, :, factor - 1, 0, :].astype(jnp.float32), axis=1)
    north_face = jnp.mean(fine_grid[:, factor - 1, :, :, 1, :].astype(jnp.float32), axis=2)
    temp_mean = jnp.mean(fine_grid[:, :, :, :, 2, :].astype(jnp.float32), axis=(1, 3))
    light_mean = jnp.mean(light_fine.reshape(row_count, factor, col_count, factor), axis=(1, 3))
    return (east_face, north_face, temp_mean, light_mean)


def open_faces(east_face, north_face, wet_cells, wet_north, wet_east):
    open_east = wet_cells * jnp.concatenate([wet_cells[:, 1:], wet_east[:, None]], axis=1)
    open_north = wet_cells * jnp.concatenate([wet_cells[1:], wet_north[None]], axis=0)
    flow_east = east_face * open_east[:, :, None]
    flow_north = north_face * open_north[:, :, None]
    return (open_east, open_north, flow_east, flow_north)


def back_faces(
    open_east,
    open_north,
    flow_east,
    flow_north,
    open_west_col,
    open_south_row,
    flow_west_col,
    flow_south_row,
):
    open_west = jnp.concatenate([open_west_col[:, None], open_east[:, :-1]], axis=1)
    open_south = jnp.concatenate([open_south_row[None], open_north[:-1]], axis=0)
    flow_west = jnp.concatenate([flow_west_col[:, None], flow_east[:, :-1]], axis=1)
    flow_south = jnp.concatenate([flow_south_row[None], flow_north[:-1]], axis=0)
    return (open_west, open_south, flow_west, flow_south)


def from_south(values, edge, side):
    return jnp.concatenate([edge, values[..., :-side]], axis=-1)


def from_north(values, edge, side):
    return jnp.concatenate([values[..., side:], edge], axis=-1)


def from_west(values, edge, side):
    shifted = jnp.concatenate([jnp.zeros_like(values[..., :1]), values[..., :-1]], axis=-1)
    column_ids = jnp.arange(side * side) % side
    return jnp.where(column_ids == 0, jnp.repeat(edge, side, axis=-1), shifted)


def from_east(values, edge, side):
    shifted = jnp.concatenate([values[..., 1:], jnp.zeros_like(values[..., :1])], axis=-1)
    column_ids = jnp.arange(side * side) % side
    return jnp.where(column_ids == side - 1, jnp.repeat(edge, side, axis=-1), shifted)


def react(mixed_cells, temp_mean, light_top, levels):

    def tracer_at(tracer_number):
        return mixed_cells[tracer_number]

    carbon_dis = tracer_at(0)
    alkalinity = tracer_at(1)
    oxygen = tracer_at(2)
    nitrate = tracer_at(3)
    ammonium = tracer_at(4)
    phosphate = tracer_at(5)
    silicate = tracer_at(6)
    iron_free = tracer_at(7)
    nano_carbon = tracer_at(8)
    diat_carbon = tracer_at(9)
    nano_chl = tracer_at(10)
    diat_chl = tracer_at(11)
    nano_iron = tracer_at(12)
    diat_iron = tracer_at(13)
    diat_silica = tracer_at(14)
    micro_zoo = tracer_at(15)
    meso_zoo = tracer_at(16)
    dissolved_org = tracer_at(17)
    small_part = tracer_at(18)
    big_part = tracer_at(19)
    small_iron = tracer_at(20)
    big_iron = tracer_at(21)
    big_silica = tracer_at(22)
    calcite = tracer_at(23)
    absorb = 0.04 + 0.02 * (positive(nano_chl) + positive(diat_chl))
    depth_sum = level_sums(absorb, levels)
    par_light = light_top[None, :] * jnp.exp(-(depth_sum + 0.5 * absorb))
    warm_factor = jnp.exp(0.0639 * temp_mean)
    nitrogen = positive(nitrate) + positive(ammonium)
    limit_nitro = nitrogen / (0.5 + nitrogen)
    limit_phos = positive(phosphate) / (0.3 + positive(phosphate))
    limit_iron = positive(iron_free) / (0.2 + positive(iron_free))
    limit_sil = positive(silicate) / (1.0 + positive(silicate))
    nutr_nano = jnp.minimum(jnp.minimum(limit_nitro, limit_phos), limit_iron)
    nutr_diat = jnp.minimum(nutr_nano, limit_sil)
    prod_nano = 0.1 * warm_factor * par_light / (par_light + 0.5) * nutr_nano * nano_carbon
    prod_diat = 0.12 * warm_factor * par_light / (par_light + 1.0) * nutr_diat * diat_carbon
    ammon_share = (positive(ammonium) + 0.01) / (nitrogen + 0.02)
    graze_nano = 0.08 * warm_factor * micro_zoo / (1.0 + positive(nano_carbon))
    graze_diat = 0.06 * warm_factor * meso_zoo / (1.0 + positive(diat_carbon))
    loss_nano = graze_nano + 0.02
    loss_diat = graze_diat + 0.02
    eaten_nano = graze_nano * nano_carbon
    eaten_diat = graze_diat * diat_carbon
    death_micro = 0.03 * micro_zoo * positive(micro_zoo)
    death_meso = 0.03 * meso_zoo * positive(meso_zoo)
    remin_doc = 0.03 * warm_factor * dissolved_org
    remin_poc = 0.02 * warm_factor * small_part
    remin_goc = 0.01 * warm_factor * big_part
    nitrify = 0.05 * ammonium
    melt_si = 0.02 * big_silica
    melt_cal = 0.01 * calcite
    melt_sfe = 0.02 * small_iron
    melt_bfe = 0.01 * big_iron
    uptake = prod_nano + prod_diat
    remin_total = remin_doc + remin_poc + remin_goc
    calcify = 0.02 * prod_nano
    updated = [
        carbon_dis + remin_total - uptake + melt_cal - calcify,
        alkalinity + 2.0 * (melt_cal - calcify) + 0.16 * ((1.0 - ammon_share) * uptake - nitrify),
        oxygen + 1.3 * (uptake - remin_total) - 0.32 * nitrify,
        nitrate + 0.16 * (nitrify - (1.0 - ammon_share) * uptake),
        ammonium + 0.16 * (remin_total - ammon_share * uptake - nitrify),
        phosphate + 0.01 * (remin_total - uptake),
        silicate + melt_si - 0.15 * prod_diat,
        iron_free + melt_sfe + melt_bfe - 0.005 * uptake,
        nano_carbon + prod_nano - loss_nano * nano_carbon,
        diat_carbon + prod_diat - loss_diat * diat_carbon,
        nano_chl + 0.03 * prod_nano - loss_nano * nano_chl,
        diat_chl + 0.03 * prod_diat - loss_diat * diat_chl,
        nano_iron + 0.005 * prod_nano - loss_nano * nano_iron,
        diat_iron + 0.005 * prod_diat - loss_diat * diat_iron,
        diat_silica + 0.15 * prod_diat - loss_diat * diat_silica,
        micro_zoo + 0.3 * eaten_nano - death_micro,
        meso_zoo + 0.3 * eaten_diat - death_meso,
        dissolved_org + 0.3 * eaten_nano + 0.02 * nano_carbon - remin_doc,
        small_part + 0.4 * eaten_nano + death_micro - remin_poc,
        big_part + 0.4 * eaten_diat + 0.02 * diat_carbon + death_meso - remin_goc,
        small_iron + loss_nano * nano_iron - melt_sfe,
        big_iron + loss_diat * diat_iron - melt_bfe,
        big_silica + loss_diat * diat_silica - melt_si,
        calcite + calcify - melt_cal,
    ]
    return jnp.stack(updated, axis=0)


def advance(current, halo_sides, physics, cell_flags, levels, tracer_count, side):
    cell_count = side * side
    sides = jnp.swapaxes(halo_sides, 1, 2)
    south_cell = from_south(current, sides[0], side).reshape(tracer_count, levels, cell_count)
    north_cell = from_north(current, sides[1], side).reshape(tracer_count, levels, cell_count)
    west_cell = from_west(current, sides[2], side).reshape(tracer_count, levels, cell_count)
    east_cell = from_east(current, sides[3], side).reshape(tracer_count, levels, cell_count)
    here = current.reshape(tracer_count, levels, cell_count)
    flow_west = physics[0:levels][None]
    flow_east = physics[levels : 2 * levels][None]
    flow_south = physics[2 * levels : 3 * levels][None]
    flow_north = physics[3 * levels : 4 * levels][None]
    temp_mean = physics[4 * levels : 5 * levels]
    mixing = physics[5 * levels : 6 * levels]
    flux_east = jnp.maximum(flow_east, 0.0) * here + jnp.minimum(flow_east, 0.0) * east_cell
    flux_west = jnp.maximum(flow_west, 0.0) * west_cell + jnp.minimum(flow_west, 0.0) * here
    flux_north = jnp.maximum(flow_north, 0.0) * here + jnp.minimum(flow_north, 0.0) * north_cell
    flux_south = jnp.maximum(flow_south, 0.0) * south_cell + jnp.minimum(flow_south, 0.0) * here
    spread = diffuse_rate * (
        cell_flags[0][None, None] * (west_cell - here)
        + cell_flags[1][None, None] * (east_cell - here)
        + cell_flags[2][None, None] * (south_cell - here)
        + cell_flags[3][None, None] * (north_cell - here)
    )
    moved_cells = here - (flux_east - flux_west) - (flux_north - flux_south) + spread
    level_index = jnp.arange(levels)[:, None]
    zero_level = jnp.zeros_like(moved_cells[:, :1])
    deeper = jnp.concatenate([moved_cells[:, 1:], zero_level], axis=1)
    shallower = jnp.concatenate([zero_level, moved_cells[:, :-1]], axis=1)
    mixing_upper = jnp.concatenate([jnp.zeros_like(mixing[:1]), mixing[:-1]], axis=0)
    flux_below = jnp.where(level_index < levels - 1, mixing[None] * (deeper - moved_cells), 0.0)
    flux_above = jnp.where(level_index > 0, mixing_upper[None] * (moved_cells - shallower), 0.0)
    mixed_cells = moved_cells + flux_below - flux_above
    reacted = react(mixed_cells, temp_mean, cell_flags[4], levels)
    return reacted.reshape(tracer_count * levels, cell_count) * cell_flags[5][None]


def shortwave(chl_levels, light_fine, wet_cells, levels, factor):
    absorb = 0.04 + 0.02 * chl_levels
    depth_sum = level_sums(absorb, levels)
    passed = (jnp.exp(-depth_sum) - jnp.exp(-(depth_sum + absorb))) * wet_cells[None]
    spread_cells = jnp.repeat(jnp.repeat(passed, factor, axis=1), factor, axis=2)
    return (light_fine[None] * spread_cells).astype(jnp.bfloat16)


def select(values, pick_rows, present):
    chosen = jnp.take(values, pick_rows, axis=0)
    keep = present.reshape((-1,) + (1,) * (chosen.ndim - 1))
    return jnp.where(keep, chosen, jnp.zeros_like(chosen))


def lat_rims(to_south, to_north):
    column_ext = extended(jnp.stack([to_south, to_north]), (("lat", 0),), 1, False)
    return (column_ext[0], column_ext[3])


def edge_rims(to_south, to_north, to_west, to_east):
    from_south_rim, from_north_rim = lat_rims(to_south, to_north)
    row_ext = extended(jnp.stack([to_west, to_east]), (("lon", 0),), 1, True)
    return (from_south_rim, from_north_rim, row_ext[0], row_ext[3])


def on_device(tracers, phys_fine, mix_coarse, surf_light, land_mask, owner_map):
    lon_count = lax.axis_size("lon")
    lon_index = lax.axis_index("lon")
    lat_index = lax.axis_index("lat")
    slot_count = tracers.shape[0]
    channels = tracers.shape[1]
    cell_count = tracers.shape[2]
    block_side = land_mask.shape[0]
    levels = mix_coarse.shape[2]
    tracer_count = channels // levels
    factor = phys_fine.shape[0] // block_side
    tile_blocks = land_mask.shape[1] // block_side
    band_row = owner_map[0]
    block_count = band_row.shape[0]
    peer_ids = jnp.arange(lon_count)
    tile_codes = lax.dynamic_slice_in_dim(band_row, lon_index * tile_blocks, tile_blocks)
    tile_wet = tile_codes >= 0
    tile_owner = jnp.where(tile_wet, tile_codes // slot_count % lon_count, 0)
    tile_match = (tile_owner[None, :] == peer_ids[:, None]) & tile_wet[None, :]
    tile_pick = jnp.sum(jnp.where(tile_match, jnp.arange(tile_blocks)[None, :], 0), axis=1)
    tile_has = jnp.any(tile_match, axis=1)
    my_codes = (lat_index * lon_count + lon_index) * slot_count + jnp.arange(slot_count)
    slot_match = band_row[None, :] == my_codes[:, None]
    slot_block = jnp.sum(jnp.where(slot_match, jnp.arange(block_count)[None, :], 0), axis=1)
    slot_full = jnp.any(slot_match, axis=1)
    slot_source = slot_block // tile_blocks
    source_match = (slot_source[None, :] == peer_ids[:, None]) & slot_full[None, :]
    owner_pick = jnp.sum(jnp.where(source_match, jnp.arange(slot_count)[None, :], 0), axis=1)
    owner_has = jnp.any(source_match, axis=1)
    west_code = jnp.take(band_row, (slot_block - 1) % block_count)
    east_code = jnp.take(band_row, (slot_block + 1) % block_count)
    west_wet = (west_code >= 0) & slot_full
    east_wet = (east_code >= 0) & slot_full
    west_slot = jnp.where(west_wet, west_code % slot_count, 0)
    east_slot = jnp.where(east_wet, east_code % slot_count, 0)

    def to_tiles(slot_values):
        outgoing = select(slot_values, owner_pick, owner_has)
        incoming = lax.all_to_all(outgoing, "lon", split_axis=0, concat_axis=0, tiled=True)
        return select(incoming, tile_owner, tile_wet)

    def to_blocks(grid_values):
        depth = grid_values.shape[-1]
        return (
            grid_values.reshape(block_side, tile_blocks, block_side, depth)
            .transpose(1, 3, 0, 2)
            .reshape(tile_blocks, depth, cell_count)
        )

    wet_cells = land_mask.astype(jnp.float32)
    east_face, north_face, temp_mean, light_mean = coarsen(phys_fine, surf_light, levels, factor)
    mix_mean = mix_coarse.astype(jnp.float32)
    wet_south, wet_north, wet_west, wet_east = edge_rims(
        wet_cells[0][:, None],
        wet_cells[-1][:, None],
        wet_cells[:, 0][:, None],
        wet_cells[:, -1][:, None],
    )
    open_east, open_north, flow_east, flow_north = open_faces(
        east_face, north_face, wet_cells, wet_north[:, 0], wet_east[:, 0]
    )
    open_west_col = wet_west[:, 0] * wet_cells[:, 0]
    open_south_row = wet_south[:, 0] * wet_cells[0]
    blank_row = jnp.zeros_like(flow_north[0])
    blank_col = jnp.zeros_like(flow_east[:, 0])
    flow_south_row, unused_north, flow_west_col, unused_east = edge_rims(
        blank_row, flow_north[-1], blank_col, flow_east[:, -1]
    )
    open_west, open_south, flow_west, flow_south = back_faces(
        open_east,
        open_north,
        flow_east,
        flow_north,
        open_west_col,
        open_south_row,
        flow_west_col,
        flow_south_row,
    )
    physics = jnp.concatenate(
        [flow_west, flow_east, flow_south, flow_north, temp_mean, mix_mean], axis=2
    )
    cell_flags = jnp.stack(
        [open_west, open_east, open_south, open_north, light_mean, wet_cells], axis=2
    )
    out_phys = select(to_blocks(physics), tile_pick, tile_has)
    out_flags = select(to_blocks(cell_flags), tile_pick, tile_has)
    got_phys, got_flags = side_by_side((out_phys, out_flags), "lon", 0, 0, 1)
    slot_phys = select(got_phys, slot_source, slot_full)
    slot_flags = select(got_flags, slot_source, slot_full)

    def advance_slot(items):
        return advance(items[0], items[1], items[2], items[3], levels, tracer_count, block_side)

    current = tracers
    for step_index in range(ITERS):
        carried = current
        edge_width = carried.shape[1]
        grid = carried.reshape(carried.shape[0], carried.shape[1], block_side, block_side)
        south_edge = jnp.swapaxes(grid[:, :, 0, :], 1, 2)
        north_edge = jnp.swapaxes(grid[:, :, -1, :], 1, 2)
        west_edge = jnp.swapaxes(grid[:, :, :, 0], 1, 2)
        east_edge = jnp.swapaxes(grid[:, :, :, -1], 1, 2)
        south_edge, north_edge, west_edge, east_edge = (
            south_edge,
            north_edge,
            west_edge,
            east_edge,
        )
        row_stack = jnp.stack([south_edge, north_edge], axis=1)
        tile_rows = to_tiles(row_stack)
        rim_south, rim_north = lat_rims(
            tile_rows[:, 0].reshape(-1, edge_width), tile_rows[:, 1].reshape(-1, edge_width)
        )
        tile_halos = jnp.stack(
            [
                rim_south.reshape(tile_blocks, block_side, edge_width),
                rim_north.reshape(tile_blocks, block_side, edge_width),
            ],
            axis=1,
        )
        halos_outgoing = select(tile_halos, tile_pick, tile_has)
        halos_incoming = lax.all_to_all(
            halos_outgoing, "lon", split_axis=0, concat_axis=0, tiled=True
        )
        slot_rows = select(halos_incoming, slot_source, slot_full)
        came_west = passed_along(east_edge, "lon", 1)
        came_east = passed_along(west_edge, "lon", -1)
        halo_west = select(came_west, west_slot, west_wet)
        halo_east = select(came_east, east_slot, east_wet)
        slot_halos = jnp.stack([slot_rows[:, 0], slot_rows[:, 1], halo_west, halo_east], axis=1)
        updated = lax.map(advance_slot, (current, slot_halos, slot_phys, slot_flags))
        current = jnp.where(slot_full[:, None, None], updated, 0.0)
    chl_slots = positive(
        current[:, nano_chl_index * levels : (nano_chl_index + 1) * levels]
    ) + positive(current[:, diat_chl_index * levels : (diat_chl_index + 1) * levels])
    tile_chl = to_tiles(chl_slots)
    chl_levels = (
        tile_chl.reshape(tile_blocks, levels, block_side, block_side)
        .transpose(1, 2, 0, 3)
        .reshape(levels, block_side, tile_blocks * block_side)
    )
    heating = shortwave(chl_levels, surf_light, wet_cells, levels, factor)
    return (current, heating)


def solution(mesh):
    in_specs = (
        P(("lat", "lon"), None, None),
        P("lat", "lon", None),
        P("lat", "lon", None),
        P("lat", "lon"),
        P("lat", "lon"),
        P("lat", None),
    )
    out_specs = (P(("lat", "lon"), None, None), P(None, "lat", "lon"))
    return jax.shard_map(
        on_device, mesh=mesh, in_specs=in_specs, out_specs=out_specs, check_vma=False
    )
```

profile of v0, /device:TPU:2, one launch (start us, length us, event | category | flops | bytes accessed | tf_op | source)
XLA Modules:
  0.0 1069.7 jit_solution(5078929205431697842)
XLA Ops:
  4.6 6.5 collective-permute-start
  14.8 9.7 copy.403
  29.0 6.8 all-to-all-start.1
  35.8 9.9 copy.390
  45.7 36.1 %reshape.724 = bf16[16,3,128,3,3,48]{5,4,3,2,1,0:T(4,128)(2,1)} reshape(bf16[48,384,144]{2,1,0:T(8,128)(2,1)} %copy.390) | data formatting | bytes 10616832 | tf_op jit(solution)/shard_map/reshape | solution.py:72
  81.7 8.8 fusion.103
  90.6 11.2 %fusion.102 = f32[16,128,48]{2,1,0:T(8,128)} fusion(bf16[16,3,128,3,3,48]{5,4,3,2,1,0:T(4,128)(2,1)} %reshape.724), kind=kLoop, calls=%fused_computation.355 | loop fusion | flops 491520 | bytes 983040 | tf_op jit(solution)/shard_map/reduce_sum | solution.py:74
  101.8 33.2 %fusion.100 = f32[16,128,48]{2,1,0:T(8,128)} fusion(bf16[16,3,128,3,3,48]{5,4,3,2,1,0:T(4,128)(2,1)} %reshape.724), kind=kLoop, calls=%fused_computation.347 | loop fusion | flops 1671168 | bytes 2162688 | tf_op jit(solution)/shard_map/reduce_sum | solution.py:75
  178.2 6.1 copy.402
  184.4 6.5 all-to-all-start
  196.3 5.2 collective-permute-start.9
  220.7 44.4 %all-to-all-done = f32[16,294,256]{2,1,0:T(8,128)} async-done(((f32[16,294,256]{2,1,0:T(8,128)}), f32[16,294,256]{2,1,0:T(8,128)}, u32[]{:S(2)}, u32[]{:S(2)}) %all-to-all-start) | async-done | bytes 4816928 | tf_op jit(solution)/shard_map/all_to_all | solution.py:34
  265.0 14.9 %all-to-all-start.2 = ((f32[16,2,16,1152]{3,2,1,0:T(8,128)}), f32[16,2,16,1152]{3,2,1,0:T(8,128)}, u32[]{:S(2)}, u32[]{:S(2)}) async-start(f32[16,2,16,1152]{3,2,1,0:T(8,128)} %select_select_fusion.3), calls=%async_computation.2 | async-start | bytes 4718592 | tf_op jit(solution)/shard_map/all_to_all | solution.py:399
  283.8 4.9 slice.851
  298.9 12.2 %all-to-all-done.2 = f32[16,2,16,1152]{3,2,1,0:T(8,128)} async-done(((f32[16,2,16,1152]{3,2,1,0:T(8,128)}), f32[16,2,16,1152]{3,2,1,0:T(8,128)}, u32[]{:S(2)}, u32[]{:S(2)}) %all-to-all-start.2) | async-done | bytes 2359328 | tf_op jit(solution)/shard_map/all_to_all | solution.py:399
  319.7 299.0 %while.24 = (s32[]{:T(128)}, f32[8,1152,256]{1,2,0:T(8,128)}, f32[8,1152,256]{2,1,0:T(8,128)}, f32[8,288,256]{2,1,0:T(8,128)}, f32[8,4,16,1152]{3,2,1,0:T(8,128)...) while((s32[]{:T(128)}, f32[8,1152,256]{1,2,0:T(8,128)}, ...), condition=%wide.region_11.16_spmd, body=%wide.region_10.15_spmd.sunk | while | flops 22468460 | bytes 66644208 | solution.py:408
  628.1 38.3 %all_to_all.30 = f32[16,2,16,1152]{3,2,1,0:T(8,128)S(1)} all-to-all(f32[16,2,16,1152]{3,2,1,0:T(8,128)S(1)} %select_select_fusion.2), channel_id=1, replica_groups=mesh['lat'=8,'lon'=16] {'lon'}, dimensions={0} | all-to-all | bytes 4718592 | tf_op jit(solution)/shard_map/all_to_all | solution.py:316
  673.2 5.6 collective-permute-done.10
  698.8 34.1 %collective-permute-done.12 = f32[8,16,1152]{2,1,0:T(8,128)S(1)} collective-permute-done((f32[8,16,1152]{2,1,0:T(8,128)S(1)}, f32[8,16,1152]{2,1,0:T(8,128)S(1)}, u32[]{:S(2)}, u32[]{:S(2)}) %collective-permute-start.12) | collective-permute-done | bytes 589856 | tf_op jit(solution)/shard_map/ppermute | solution.py:46
  745.5 272.6 %while.25 = (s32[]{:T(128)}, f32[8,1152,256]{1,2,0:T(8,128)}, f32[8,1152,256]{1,2,0:T(8,128)}, f32[8,288,256]{2,1,0:T(8,128)}, f32[8,4,16,1152]{3,2,1,0:T(8,128)...) while((s32[]{:T(128)}, f32[8,1152,256]{1,2,0:T(8,128)}, ...), condition=%wide.region_13.18_spmd, body=%wide.region_12.17_spmd.sunk | while | flops 22468460 | bytes 68118720 | solution.py:408
  1032.3 6.5 all-to-all-start.5
  1039.0 9.6 copy.425
  1048.6 5.4 all-to-all-done.5
  1063.1 6.3 copy.426
  (1251 shorter events, 741.4 us)
Async XLA Ops:
  1.3 144.8 %copy-start.15 = (f32[16,128]{1,0:T(8,128)}, f32[16,128]{1,0:T(8,128)S(1)}, u32[]{:S(2)}) copy-start(f32[16,128]{1,0:T(8,128)S(1)} %convert_element_type.25) | copy-start | bytes 24580
  1.9 140.7 %collective-permute-start.5 = (f32[1,128,1]{1,2,0:T(1,128)}, f32[1,128,1]{1,2,0:T(1,128)}, u32[]{:S(2)}, u32[]{:S(2)}) collective-permute-start(f32[1,128,1]{1,2,0:T(1,128)} %slice_bitcast_fusion.30), channel_id=1, source_target_pairs={{0,16},{16,32},{32,48},{48,64},{64,80},{80,96},{96,112},{1,17},{17... | collective-permute-start | bytes 1544 | tf_op jit(solution)/shard_map/ppermute | solution.py:22
  4.6 141.5 %collective-permute-start = (f32[1,16,1]{1,2,0:T(1,128)}, f32[1,16,1]{1,2,0:T(1,128)}, u32[]{:S(2)}, u32[]{:S(2)}) collective-permute-start(f32[1,16,1]{1,2,0:T(1,128)} %bitcast.225), channel_id=1, source_target_pairs={{1,0},{2,1},{3,2},{4,3},{5,4},{6,5},{7,6},{8,7},{9,8},{10,9},{11,1... | collective-permute-start | bytes 200 | tf_op jit(solution)/shard_map/ppermute | solution.py:24
  11.1 130.8 %collective-permute-start.4 = (f32[1,16,1]{1,2,0:T(1,128)}, f32[1,16,1]{1,2,0:T(1,128)}, u32[]{:S(2)}, u32[]{:S(2)}) collective-permute-start(f32[1,16,1]{1,2,0:T(1,128)} %bitcast.227), channel_id=1, source_target_pairs={{0,1},{1,2},{2,3},{3,4},{4,5},{5,6},{6,7},{7,8},{8,9},{9,10},{10,1... | collective-permute-start | bytes 200 | tf_op jit(solution)/shard_map/ppermute | solution.py:22
  12.8 300.6 %copy-start.23 = (pred[8]{0:T(512)(128)(4,1)}, pred[8]{0:T(512)(128)(4,1)S(1)}, u32[]{:S(2)}) copy-start(pred[8]{0:T(512)(128)(4,1)S(1)} %compare_reduce_fusion) | copy-start | bytes 28
  29.0 155.4 %all-to-all-start.1 = ((f32[16,2,16,1152]{3,2,1,0:T(8,128)}), f32[16,2,16,1152]{3,2,1,0:T(8,128)}, u32[]{:S(2)}, u32[]{:S(2)}) async-start(f32[16,2,16,1152]{3,2,1,0:T(8,128)} %select_select_fusion.4), calls=%async_computation.1 | async-start | bytes 4718592 | tf_op jit(solution)/shard_map/all_to_all | solution.py:316
  135.8 83.1 %copy-start.25 = (pred[16]{0:T(512)(128)(4,1)}, pred[16]{0:T(512)(128)(4,1)S(1)}, u32[]{:S(2)}) copy-start(pred[16]{0:T(512)(128)(4,1)S(1)} %compare_and_fusion.6) | copy-start | bytes 52
  143.3 4.1 collective-permute-start.2
  147.9 8.3 collective-permute-start.1
  149.5 8.7 collective-permute-start.3
  184.4 80.7 %all-to-all-start = ((f32[16,294,256]{2,1,0:T(8,128)}), f32[16,294,256]{2,1,0:T(8,128)}, u32[]{:S(2)}, u32[]{:S(2)}) async-start(f32[16,294,256]{2,1,0:T(8,128)} %copy.402), calls=%async_computation | async-start | bytes 9699328 | tf_op jit(solution)/shard_map/all_to_all | solution.py:34
  196.3 83.8 %collective-permute-start.9 = (f32[8,16,1152]{2,1,0:T(8,128)}, f32[8,16,1152]{2,1,0:T(8,128)}, u32[]{:S(2)}, u32[]{:S(2)}) collective-permute-start(f32[8,16,1152]{2,1,0:T(8,128)} %bitcast.815), channel_id=1, source_target_pairs={{0,15},{1,0},{2,1},{3,2},{4,3},{5,4},{6,5},{7,6},{8,7},{9,8},{10,9... | collective-permute-start | bytes 1769480 | tf_op jit(solution)/shard_map/ppermute | solution.py:46
  202.4 79.4 %collective-permute-start.8 = (f32[8,16,1152]{2,1,0:T(8,128)}, f32[8,16,1152]{2,1,0:T(8,128)}, u32[]{:S(2)}, u32[]{:S(2)}) collective-permute-start(f32[8,16,1152]{2,1,0:T(8,128)} %bitcast.816), channel_id=1, source_target_pairs={{0,1},{1,2},{2,3},{3,4},{4,5},{5,6},{6,7},{7,8},{8,9},{9,10},{10,1... | collective-permute-start | bytes 1769480 | tf_op jit(solution)/shard_map/ppermute | solution.py:46
  205.1 11.2 %collective-permute-start.6 = (f32[1,128,1152]{2,1,0:T(8,128)S(1)}, f32[1,128,1152]{2,1,0:T(8,128)S(1)}, u32[]{:S(2)}, u32[]{:S(2)}) collective-permute-start(f32[1,128,1152]{2,1,0:T(8,128)S(1)} %bitcast.1122), channel_id=1, source_target_pairs={{0,16},{16,32},{32,48},{48,64},{64,80},{80,96},{96,112},{1,17},{17... | collective-permute-start | bytes 1769480 | tf_op jit(solution)/shard_map/ppermute | solution.py:22
  207.0 11.0 %collective-permute-start.7 = (f32[1,128,1152]{2,1,0:T(8,128)S(1)}, f32[1,128,1152]{2,1,0:T(8,128)S(1)}, u32[]{:S(2)}, u32[]{:S(2)}) collective-permute-start(f32[1,128,1152]{2,1,0:T(8,128)S(1)} %bitcast.1120), channel_id=1, source_target_pairs={{16,0},{32,16},{48,32},{64,48},{80,64},{96,80},{112,96},{17,1},{33... | collective-permute-start | bytes 1769480 | tf_op jit(solution)/shard_map/ppermute | solution.py:24
  220.7 59.4 %copy-start.60 = (s32[8]{0:T(128)S(1)}, s32[8]{0:T(128)}, u32[]{:S(2)}) copy-start(s32[8]{0:T(128)} %get-tuple-element.323) | copy-start | bytes 100
  220.7 59.4 %copy-start.63 = (s32[8]{0:T(128)S(1)}, s32[8]{0:T(128)}, u32[]{:S(2)}) copy-start(s32[8]{0:T(128)} %copy-done.62) | copy-start | bytes 100
  265.0 46.0 %all-to-all-start.2 = ((f32[16,2,16,1152]{3,2,1,0:T(8,128)}), f32[16,2,16,1152]{3,2,1,0:T(8,128)}, u32[]{:S(2)}, u32[]{:S(2)}) async-start(f32[16,2,16,1152]{3,2,1,0:T(8,128)} %select_select_fusion.3), calls=%async_computation.2 | async-start | bytes 4718592 | tf_op jit(solution)/shard_map/all_to_all | solution.py:399
  667.6 11.2 %collective-permute-start.10 = (f32[1,128,1152]{2,1,0:T(8,128)S(1)}, f32[1,128,1152]{2,1,0:T(8,128)S(1)}, u32[]{:S(2)}, u32[]{:S(2)}) collective-permute-start(f32[1,128,1152]{2,1,0:T(8,128)S(1)} %bitcast.1126), channel_id=1, source_target_pairs={{0,16},{16,32},{32,48},{48,64},{64,80},{80,96},{96,112},{1,17},{17... | collective-permute-start | bytes 1769480 | tf_op jit(solution)/shard_map/ppermute | solution.py:22
  669.5 11.0 %collective-permute-start.11 = (f32[1,128,1152]{2,1,0:T(8,128)S(1)}, f32[1,128,1152]{2,1,0:T(8,128)S(1)}, u32[]{:S(2)}, u32[]{:S(2)}) collective-permute-start(f32[1,128,1152]{2,1,0:T(8,128)S(1)} %bitcast.1124), channel_id=1, source_target_pairs={{16,0},{32,16},{48,32},{64,48},{80,64},{96,80},{112,96},{17,1},{33... | collective-permute-start | bytes 1769480 | tf_op jit(solution)/shard_map/ppermute | solution.py:24
  683.3 54.0 %all-to-all-start.4 = ((f32[16,2,16,1152]{3,2,1,0:T(8,128)}), f32[16,2,16,1152]{3,2,1,0:T(8,128)S(1)}, u32[]{:S(2)}, u32[]{:S(2)}) async-start(f32[16,2,16,1152]{3,2,1,0:T(8,128)} %select_select_fusion.1), calls=%async_computation.4 | async-start | bytes 4718592 | tf_op jit(solution)/shard_map/all_to_all | solution.py:399
  691.9 41.0 %collective-permute-start.12 = (f32[8,16,1152]{2,1,0:T(8,128)S(1)}, f32[8,16,1152]{2,1,0:T(8,128)S(1)}, u32[]{:S(2)}, u32[]{:S(2)}) collective-permute-start(f32[8,16,1152]{2,1,0:T(8,128)S(1)} %bitcast.1119), channel_id=1, source_target_pairs={{0,1},{1,2},{2,3},{3,4},{4,5},{5,6},{6,7},{7,8},{8,9},{9,10},{10,1... | collective-permute-start | bytes 1769480 | tf_op jit(solution)/shard_map/ppermute | solution.py:46
  694.7 38.9 %collective-permute-start.13 = (f32[8,16,1152]{2,1,0:T(8,128)}, f32[8,16,1152]{2,1,0:T(8,128)}, u32[]{:S(2)}, u32[]{:S(2)}) collective-permute-start(f32[8,16,1152]{2,1,0:T(8,128)} %bitcast.813), channel_id=1, source_target_pairs={{0,15},{1,0},{2,1},{3,2},{4,3},{5,4},{6,5},{7,6},{8,7},{9,8},{10,9... | collective-permute-start | bytes 1769480 | tf_op jit(solution)/shard_map/ppermute | solution.py:46
  1032.3 21.6 %all-to-all-start.5 = ((f32[16,48,256]{2,1,0:T(8,128)}), f32[16,48,256]{2,1,0:T(8,128)S(1)}, u32[]{:S(2)}, u32[]{:S(2)}) async-start(f32[16,48,256]{2,1,0:T(8,128)} %copy.417), calls=%async_computation.5 | async-start | bytes 1572864 | tf_op jit(solution)/shard_map/all_to_all | solution.py:316
  (121 other events, 651.0 us)
where the time goes:
time: 1090 us; the launch traced here: 1070 us
  local copies, waits for them, and re-layouts  502 us (46%)
  other arithmetic  321 us (29%)
  waiting for transfers between devices  109 us (10%)
  starting transfers between devices  76.4 us (7%)
  blocking collectives  38.3 us (4%)
  matrix products  17 us (2%)
    while x352, other arithmetic  98.8 us
    dynamic_slice x64, local copies, waits for them, and re-layouts, on_device(): lax.map(advance_slot, (current, slot_halos, slot_phys, slot_flags))  61.9 us
    slice x32, local copies, waits for them, and re-layouts, from_north(): return jnp.concatenate([values[..., side:], edge], axis=-1)  57.5 us
    add x16, other arithmetic, advance(): here - (flux_east - flux_west) - (flux_north - flux_south) + spread  56.6 us
    unnamed x136, local copies, waits for them, and re-layouts  47.2 us
    all_to_all x1, waiting for transfers between devices, side_by_side(): lax.all_to_all(both, axis, split_axis=split_dim, concat_axis=concat_dim,...  44.4 us
    slice x16, local copies, waits for them, and re-layouts, from_south(): return jnp.concatenate([edge, values[..., :-side]], axis=-1)  42.8 us
    all_to_all x1, blocking collectives, to_tiles(): lax.all_to_all(outgoing, 'lon', split_axis=0, concat_axis=0, tiled=True)  38.3 us
  transfers between devices with their start and end apart: 19, of which 9 were waited for; matrix products, arithmetic and copies ran while one was open for 20% of the time, Pallas kernels for 0%

commit v1 on v0

v1 whole, which is shorter than its diff:
```python
import functools

import jax
import jax.numpy as jnp
from jax import lax
from jax.experimental import pallas as pl
from jax.experimental.pallas import tpu as pltpu
from jax.sharding import PartitionSpec as P

NTR = 24
LEV = 48
SIDE = 16
CELLS = 256
SLOTS = 8
TILE = 8
PHYS = 224
DIFF = 0.08
VM = pltpu.VMEM
ROWS3 = 3 * LEV


def pos(v):
    return jnp.maximum(v, 0.0)


def lanes():
    return lax.broadcasted_iota(jnp.int32, (LEV, 128), 1)


def roll(x, shift):
    return pltpu.roll(x, shift, 1)


def pack_edges(c_ref, rows_ref, w_ref, e_ref, odd):
    lane = lanes()
    group = lane // SIDE
    col = lane % SIDE
    base = odd * 8
    for m in range(3):
        blank = jnp.zeros((LEV, 128), jnp.float32)
        south, north = blank, blank
        west, east = [blank, blank], [blank, blank]
        for g in range(8):
            t = 3 * g + m
            a = c_ref[0, t * LEV:(t + 1) * LEV, 0:128]
            b = c_ref[0, t * LEV:(t + 1) * LEV, 128:256]
            south = jnp.where(group == g, roll(a, 16 * g) if g else a, south)
            north = jnp.where(group == g, roll(b, (16 * g + 16) % 128), north)
            for h, v in enumerate((a, b)):
                west[h] = jnp.where(col == g, roll(v, g) if g else v, west[h])
                east[h] = jnp.where(col == g, roll(v, (g - 15) % 128), east[h])
        at = slice(m * LEV, (m + 1) * LEV)
        rows_ref[0, 0, at, :] = south
        rows_ref[0, 1, at, :] = north
        mine = (col // 8) == odd
        for h in range(2):
            hs = slice(h * 128, (h + 1) * 128)
            w_ref[0, at, hs] = jnp.where(mine, roll(west[h], base), w_ref[0, at, hs])
            e_ref[0, at, hs] = jnp.where(mine, roll(east[h], base), e_ref[0, at, hs])


def clear_first(odd, *refs):
    @pl.when(odd == 0)
    def _():
        for ref in refs:
            ref[...] = jnp.zeros_like(ref)


def pack_kernel(tab, c_ref, rows_ref, w_ref, e_ref):
    odd = pl.program_id(0) % 2
    clear_first(odd, w_ref, e_ref)
    pack_edges(c_ref, rows_ref, w_ref, e_ref, odd)


def pack(tab, tracers):
    return pl.pallas_call(
        pack_kernel,
        grid_spec=pltpu.PrefetchScalarGridSpec(
            num_scalar_prefetch=1,
            grid=(SLOTS,),
            in_specs=[pl.BlockSpec((1, NTR * LEV, CELLS), lambda j, tab: (j, 0, 0))],
            out_specs=[
                pl.BlockSpec((1, 2, ROWS3, 128), lambda j, tab: (tab[4, j], 0, 0, 0)),
                pl.BlockSpec((1, ROWS3, CELLS), lambda j, tab: (j // 2, 0, 0)),
                pl.BlockSpec((1, ROWS3, CELLS), lambda j, tab: (j // 2, 0, 0)),
            ],
        ),
        out_shape=[
            jax.ShapeDtypeStruct((16, 2, ROWS3, 128), jnp.float32),
            jax.ShapeDtypeStruct((4, ROWS3, CELLS), jnp.float32),
            jax.ShapeDtypeStruct((4, ROWS3, CELLS), jnp.float32),
        ],
        cost_estimate=pl.CostEstimate(flops=10**7, bytes_accessed=12 * 10**6, transcendentals=0),
        name="pack",
    )(tab, tracers)


def react(get, put, par, warm):
    (carbon_dis, alkalinity, oxygen, nitrate, ammonium, phosphate, silicate, iron_free,
     nano_carbon, diat_carbon, nano_chl, diat_chl, nano_iron, diat_iron, diat_silica,
     micro_zoo, meso_zoo, dissolved_org, small_part, big_part, small_iron, big_iron,
     big_silica, calcite) = [functools.partial(get, t) for t in range(NTR)]
    p_am = pos(ammonium())
    nitrogen = pos(nitrate()) + p_am
    limit_nitro = nitrogen / (0.5 + nitrogen)
    p_ph = pos(phosphate())
    p_fe = pos(iron_free())
    p_si = pos(silicate())
    nutr_nano = jnp.minimum(jnp.minimum(limit_nitro, p_ph / (0.3 + p_ph)), p_fe / (0.2 + p_fe))
    nutr_diat = jnp.minimum(nutr_nano, p_si / (1.0 + p_si))
    nc = nano_carbon()
    dc = diat_carbon()
    wp = warm * par
    prod_nano = 0.1 * wp / (par + 0.5) * nutr_nano * nc
    prod_diat = 0.12 * wp / (par + 1.0) * nutr_diat * dc
    share = (p_am + 0.01) / (nitrogen + 0.02)
    mi = micro_zoo()
    me = meso_zoo()
    graze_nano = 0.08 * warm * mi / (1.0 + pos(nc))
    graze_diat = 0.06 * warm * me / (1.0 + pos(dc))
    loss_nano = graze_nano + 0.02
    loss_diat = graze_diat + 0.02
    eaten_nano = graze_nano * nc
    eaten_diat = graze_diat * dc
    death_micro = 0.03 * mi * pos(mi)
    death_meso = 0.03 * me * pos(me)
    do = dissolved_org()
    sp = small_part()
    bp = big_part()
    remin_doc = 0.03 * warm * do
    remin_poc = 0.02 * warm * sp
    remin_goc = 0.01 * warm * bp
    am = ammonium()
    nitrify = 0.05 * am
    cal = calcite()
    melt_cal = 0.01 * cal
    uptake = prod_nano + prod_diat
    remin = remin_doc + remin_poc + remin_goc
    calcify = 0.02 * prod_nano
    shell = melt_cal - calcify
    put(0, carbon_dis() + remin - uptake + shell)
    su = share * uptake
    fresh = uptake - su
    put(1, alkalinity() + 2.0 * shell + 0.16 * (fresh - nitrify))
    put(2, oxygen() + 1.3 * (uptake - remin) - 0.32 * nitrify)
    put(3, nitrate() + 0.16 * (nitrify - fresh))
    put(4, am + 0.16 * (remin - su - nitrify))
    put(5, phosphate() + 0.01 * (remin - uptake))
    bsi = big_silica()
    melt_si = 0.02 * bsi
    put(6, silicate() + melt_si - 0.15 * prod_diat)
    sfe = small_iron()
    bfe = big_iron()
    melt_sfe = 0.02 * sfe
    melt_bfe = 0.01 * bfe
    put(7, iron_free() + melt_sfe + melt_bfe - 0.005 * uptake)
    put(8, nc + prod_nano - loss_nano * nc)
    put(9, dc + prod_diat - loss_diat * dc)
    x = nano_chl()
    put(10, x + 0.03 * prod_nano - loss_nano * x)
    x = diat_chl()
    put(11, x + 0.03 * prod_diat - loss_diat * x)
    x = nano_iron()
    lost = loss_nano * x
    put(12, x + 0.005 * prod_nano - lost)
    put(20, sfe + lost - melt_sfe)
    x = diat_iron()
    lost = loss_diat * x
    put(13, x + 0.005 * prod_diat - lost)
    put(21, bfe + lost - melt_bfe)
    x = diat_silica()
    lost = loss_diat * x
    put(14, x + 0.15 * prod_diat - lost)
    put(22, bsi + lost - melt_si)
    put(15, mi + 0.3 * eaten_nano - death_micro)
    put(16, me + 0.3 * eaten_diat - death_meso)
    put(17, do + 0.3 * eaten_nano + 0.02 * nc - remin_doc)
    put(18, sp + 0.4 * eaten_nano + death_micro - remin_poc)
    put(19, bp + 0.4 * eaten_diat + 0.02 * dc + death_meso - remin_goc)
    put(23, cal - shell)


def tri():
    i = lax.broadcasted_iota(jnp.int32, (LEV, LEV), 0)
    j = lax.broadcasted_iota(jnp.int32, (LEV, LEV), 1)
    return (j < i).astype(jnp.float32)


def depth(absorb):
    return jnp.dot(tri(), absorb, precision=lax.Precision.HIGHEST,
                   preferred_element_type=jnp.float32)


def slot_step(tab, c_ref, phys, rows, west, east, out, coef, par_ref):
    j = pl.program_id(0)
    w_odd = tab[2, j] % 2
    e_odd = tab[3, j] % 2
    lane = lanes()
    col = lane % SIDE
    at_w = col == 0
    at_e = col == SIDE - 1
    low = lane < 16
    high = lane >= 112
    H = (slice(0, 128), slice(128, 256))
    edge = jnp.concatenate([phys[0, 200:224, 0:128], phys[0, 200:224, 128:256]], axis=0)
    sel_r = lax.broadcasted_iota(jnp.int32, (128, 256), 0)
    sel_c = lax.broadcasted_iota(jnp.int32, (128, 256), 1)
    sel = ((sel_c == SIDE * sel_r) & (sel_r < SIDE)).astype(jnp.float32)
    edge_lane = jnp.where(low, edge, 0.0)
    edge_w = jnp.dot(edge_lane, sel, precision=lax.Precision.HIGHEST,
                     preferred_element_type=jnp.float32)
    edge_s = roll(edge, 112)
    fn_up = roll(phys[0, 48:96, H[0]], 16)
    level = lax.broadcasted_iota(jnp.int32, (LEV, 128), 0)
    for h in range(2):
        fe = phys[0, 0:48, H[h]]
        fn = phys[0, 48:96, H[h]]
        fw = jnp.where(at_w, edge_w[:, H[h]], roll(fe, 1))
        if h == 0:
            fs = jnp.where(low, edge_s, fn_up)
        else:
            fs = jnp.where(low, fn_up, roll(fn, 16))
        ow = DIFF * phys[0, 192:193, H[h]]
        oe = DIFF * phys[0, 193:194, H[h]]
        os = DIFF * phys[0, 194:195, H[h]]
        on = DIFF * phys[0, 195:196, H[h]]
        coef[0, :, H[h]] = (1.0 - (ow + oe + os + on)) - pos(fe) + jnp.minimum(fw, 0.0) - pos(fn) + jnp.minimum(fs, 0.0)
        coef[1, :, H[h]] = oe - jnp.minimum(fe, 0.0)
        coef[2, :, H[h]] = ow + pos(fw)
        coef[3, :, H[h]] = on - jnp.minimum(fn, 0.0)
        coef[4, :, H[h]] = os + pos(fs)
        coef[5, :, H[h]] = jnp.where(level < LEV - 1, phys[0, 144:192, H[h]], 0.0)

    def mix(moved, k):
        flux = k * (pltpu.roll(moved, LEV - 1, 0) - moved)
        return moved + flux - pltpu.roll(flux, 1, 0)

    def group(g, carry):
        for m in range(3):
            at = pl.ds(pl.multiple_of((3 * g + m) * LEV, LEV), LEV)
            hm = slice(m * LEV, (m + 1) * LEV)
            a = c_ref[0, at, H[0]]
            b = c_ref[0, at, H[1]]
            hs = roll(rows[0, 0, hm, :], (128 - 16 * g) % 128)
            hn = roll(rows[0, 1, hm, :], 112 - 16 * g)
            an, bn = roll(a, 112), roll(b, 112)
            as_, bs = roll(a, 16), roll(b, 16)
            north = (jnp.where(high, bn, an), jnp.where(high, hn, bn))
            south = (jnp.where(low, hs, as_), jnp.where(low, as_, bs))
            w_shift = (128 - (8 * w_odd + g)) % 128
            e_shift = 15 - (8 * e_odd + g)
            for h, v in enumerate((a, b)):
                vw = jnp.where(at_w, roll(west[0, hm, H[h]], w_shift), roll(v, 1))
                ve = jnp.where(at_e, roll(east[0, hm, H[h]], e_shift), roll(v, 127))
                moved = (coef[0, :, H[h]] * v + coef[1, :, H[h]] * ve + coef[2, :, H[h]] * vw
                         + coef[3, :, H[h]] * north[h] + coef[4, :, H[h]] * south[h])
                out[0, at, H[h]] = mix(moved, coef[5, :, H[h]])
        return carry

    lax.fori_loop(0, 8, group, 0)
    absorb = 0.04 + 0.02 * (pos(out[0, 480:528, :]) + pos(out[0, 528:576, :]))
    above = depth(absorb)
    par_ref[...] = phys[0, 196:197, :] * jnp.exp(-(above + 0.5 * absorb))
    for h in range(2):
        wet = jnp.broadcast_to(phys[0, 197:198, H[h]], (8, 128))

        def chunk(i, carry):
            l0 = pl.multiple_of(i * 8, 8)

            def get(t):
                return out[0, pl.ds(pl.multiple_of(t * LEV + l0, 8), 8), H[h]]

            held = [get(t) for t in range(NTR)]

            def put(t, v):
                out[0, pl.ds(pl.multiple_of(t * LEV + l0, 8), 8), H[h]] = v * wet

            warm = jnp.exp(0.0639 * phys[0, pl.ds(pl.multiple_of(96 + l0, 8), 8), H[h]])
            par = par_ref[pl.ds(l0, 8), H[h]]
            react(lambda t: held[t], put, par, warm)
            return carry

        lax.fori_loop(0, LEV // 8, chunk, 0)


def first_kernel(tab, c_ref, phys, rows, west, east, out, rows_out, w_out, e_out, coef, par_ref):
    j = pl.program_id(0)
    odd = j % 2

    @pl.when(tab[1, j] == 1)
    def _():
        slot_step(tab, c_ref, phys, rows, west, east, out, coef, par_ref)

    @pl.when(tab[1, j] == 0)
    def _():
        out[...] = jnp.zeros_like(out)

    clear_first(odd, w_out, e_out)
    pack_edges(out, rows_out, w_out, e_out, odd)


def last_kernel(tab, c_ref, phys, rows, west, east, out, light_out, coef, par_ref):
    j = pl.program_id(0)

    @pl.when(tab[1, j] == 1)
    def _():
        slot_step(tab, c_ref, phys, rows, west, east, out, coef, par_ref)
        absorb = 0.04 + 0.02 * (pos(out[0, 480:528, :]) + pos(out[0, 528:576, :]))
        above = depth(absorb)
        light_out[0] = jnp.exp(-above) - jnp.exp(-(above + absorb))

    @pl.when(tab[1, j] == 0)
    def _():
        out[...] = jnp.zeros_like(out)
        light_out[...] = jnp.zeros_like(light_out)


def step(last, tab, current, phys, rows, came_west, came_east):
    edge_spec = pl.BlockSpec((1, ROWS3, CELLS), lambda j, tab: (j // 2, 0, 0))
    edge_shape = jax.ShapeDtypeStruct((4, ROWS3, CELLS), jnp.float32)
    if last:
        outs = [pl.BlockSpec((1, LEV, CELLS), lambda j, tab: (tab[4, j], 0, 0))]
        shapes = [jax.ShapeDtypeStruct((16, LEV, CELLS), jnp.float32)]
    else:
        outs = [pl.BlockSpec((1, 2, ROWS3, 128), lambda j, tab: (tab[4, j], 0, 0, 0)), edge_spec, edge_spec]
        shapes = [jax.ShapeDtypeStruct((16, 2, ROWS3, 128), jnp.float32), edge_shape, edge_shape]
    return pl.pallas_call(
        last_kernel if last else first_kernel,
        grid_spec=pltpu.PrefetchScalarGridSpec(
            num_scalar_prefetch=1,
            grid=(SLOTS,),
            in_specs=[
                pl.BlockSpec((1, NTR * LEV, CELLS), lambda j, tab: (j, 0, 0)),
                pl.BlockSpec((1, PHYS, CELLS), lambda j, tab: (tab[0, j], 0, 0)),
                pl.BlockSpec((1, 2, ROWS3, 128), lambda j, tab: (tab[0, j], 0, 0, 0)),
                pl.BlockSpec((1, ROWS3, CELLS), lambda j, tab: (tab[2, j] // 2, 0, 0)),
                pl.BlockSpec((1, ROWS3, CELLS), lambda j, tab: (tab[3, j] // 2, 0, 0)),
            ],
            out_specs=[pl.BlockSpec((1, NTR * LEV, CELLS), lambda j, tab: (j, 0, 0))] + outs,
            scratch_shapes=[VM((6, LEV, CELLS), jnp.float32), VM((LEV, CELLS), jnp.float32)],
        ),
        out_shape=[jax.ShapeDtypeStruct((SLOTS, NTR * LEV, CELLS), jnp.float32)] + shapes,
        cost_estimate=pl.CostEstimate(flops=10**8, bytes_accessed=25 * 10**6, transcendentals=10**6),
        name="last_step" if last else "first_step",
    )(tab, current, phys, rows, came_west, came_east)


def spread_matrix(shape, lhs_wide, dtype=jnp.bfloat16):
    i = lax.broadcasted_iota(jnp.int32, shape, 0)
    j = lax.broadcasted_iota(jnp.int32, shape, 1)
    return (i // 3 == j if lhs_wide else i == j // 3).astype(dtype)


def coarse_kernel(phys, mix, flags, y_ref, col_ref):
    r = pl.program_id(0)
    i = lax.broadcasted_iota(jnp.int32, (384, 128), 0)
    j = lax.broadcasted_iota(jnp.int32, (384, 128), 1)
    every = (i // 3 == j).astype(jnp.bfloat16)
    third = (i == 3 * j + 2).astype(jnp.bfloat16)

    def dot(a, b):
        return jnp.dot(a, b, preferred_element_type=jnp.float32)

    east = (dot(phys[0, 0:48, :], third) + dot(phys[1, 0:48, :], third) + dot(phys[2, 0:48, :], third)) / 3.0
    north = dot(phys[2, 48:96, :], every) / 3.0
    temp = (dot(phys[0, 96:144, :], every) + dot(phys[1, 96:144, :], every) + dot(phys[2, 96:144, :], every)) / 9.0
    east = east * flags[0, 1:2, :]
    y_ref[0, 0:48, :] = east
    y_ref[0, 48:96, :] = north * flags[0, 3:4, :]
    y_ref[0, 96:144, :] = temp
    y_ref[0, 144:192, :] = mix[0].astype(jnp.float32)
    y_ref[0, 192:200, :] = flags[0]

    @pl.when(r == 0)
    def _():
        col_ref[...] = jnp.zeros_like(col_ref)

    col_ref[...] = jnp.where(lanes() == r, roll(east, r + 1), col_ref[...])


def coarse(phys_t, mix_t, flags):
    return pl.pallas_call(
        coarse_kernel,
        grid=(SIDE,),
        in_specs=[
            pl.BlockSpec((3, 144, 384), lambda r: (r, 0, 0)),
            pl.BlockSpec((1, LEV, 128), lambda r: (r, 0, 0)),
            pl.BlockSpec((1, 8, 128), lambda r: (r, 0, 0)),
        ],
        out_specs=[
            pl.BlockSpec((1, 200, 128), lambda r: (r, 0, 0)),
            pl.BlockSpec((LEV, 128), lambda r: (0, 0)),
        ],
        out_shape=[
            jax.ShapeDtypeStruct((SIDE, 200, 128), jnp.float32),
            jax.ShapeDtypeStruct((LEV, 128), jnp.float32),
        ],
        cost_estimate=pl.CostEstimate(flops=10**9, bytes_accessed=8 * 10**6, transcendentals=0),
        name="coarse",
    )(phys_t, mix_t, flags)


def package_kernel(tab, y_ref, col_ref, row_ref, out):
    k = pl.program_id(0)
    lane = lanes()
    group = lane // SIDE
    for f in range(5):
        n = 48 if f < 4 else 8
        at = slice(48 * f, 48 * f + n)
        for h in range(2):
            acc = jnp.zeros((n, 128), jnp.float32)
            for g in range(8):
                turned = roll(y_ref[8 * h + g, at, :], (16 * g - 16 * k + 128) % 128)
                acc = jnp.where(group[:n] == g, turned, acc)
            out[0, at, 128 * h:128 * h + 128] = acc
    west = col_ref[...]
    for r in range(SIDE):
        turned = roll(y_ref[r, 0:48, :], (r + 1 - 16 * k + 128) % 128)
        west = jnp.where((lane == r) & (k > 0), turned, west)
    edge = jnp.where(lane < 16, west, roll(row_ref[...], (16 - 16 * k + 128) % 128))
    out[0, 200:224, 0:128] = edge[0:24]
    out[0, 200:224, 128:256] = edge[24:48]


def package(tab, y, col, row):
    return pl.pallas_call(
        package_kernel,
        grid_spec=pltpu.PrefetchScalarGridSpec(
            num_scalar_prefetch=1,
            grid=(TILE,),
            in_specs=[
                pl.BlockSpec((SIDE, 200, 128), lambda k, tab: (0, 0, 0)),
                pl.BlockSpec((LEV, 128), lambda k, tab: (0, 0)),
                pl.BlockSpec((LEV, 128), lambda k, tab: (0, 0)),
            ],
            out_specs=pl.BlockSpec((1, PHYS, CELLS), lambda k, tab: (tab[6, k], 0, 0)),
        ),
        out_shape=jax.ShapeDtypeStruct((16, PHYS, CELLS), jnp.float32),
        cost_estimate=pl.CostEstimate(flops=10**7, bytes_accessed=4 * 10**6, transcendentals=0),
        name="package",
    )(tab, y, col, row)


def unpick_kernel(tab, got, south, north):
    wet = tab[5, pl.program_id(0)] == 1
    south[0] = jnp.where(wet, got[0, 0], 0.0)
    north[0] = jnp.where(wet, got[0, 1], 0.0)


def unpick(tab, got):
    one = pl.BlockSpec((1, ROWS3, 128), lambda k, tab: (k, 0, 0))
    return pl.pallas_call(
        unpick_kernel,
        grid_spec=pltpu.PrefetchScalarGridSpec(
            num_scalar_prefetch=1,
            grid=(TILE,),
            in_specs=[pl.BlockSpec((1, 2, ROWS3, 128), lambda k, tab: (tab[6, k], 0, 0, 0))],
            out_specs=[one, one],
        ),
        out_shape=[jax.ShapeDtypeStruct((TILE, ROWS3, 128), jnp.float32)] * 2,
        cost_estimate=pl.CostEstimate(flops=10**6, bytes_accessed=24 * 10**5, transcendentals=0),
        name="unpick",
    )(tab, got)


def repick_kernel(tab, south, north, out):
    out[0, 0] = south[0]
    out[0, 1] = north[0]


def repick(tab, south, north):
    one = pl.BlockSpec((1, ROWS3, 128), lambda k, tab: (k, 0, 0))
    return pl.pallas_call(
        repick_kernel,
        grid_spec=pltpu.PrefetchScalarGridSpec(
            num_scalar_prefetch=1,
            grid=(TILE,),
            in_specs=[one, one],
            out_specs=pl.BlockSpec((1, 2, ROWS3, 128), lambda k, tab: (tab[6, k], 0, 0, 0)),
        ),
        out_shape=jax.ShapeDtypeStruct((16, 2, ROWS3, 128), jnp.float32),
        cost_estimate=pl.CostEstimate(flops=10**6, bytes_accessed=24 * 10**5, transcendentals=0),
        name="repick",
    )(tab, south, north)


def heat_kernel(tab, got, wet, light, out, fine):
    lane = lanes()
    group = lane // SIDE
    for r in range(SIDE):
        half = slice(128 * (r // 8), 128 * (r // 8) + 128)
        acc = jnp.zeros((LEV, 128), jnp.float32)
        for k in range(TILE):
            acc = jnp.where(group == k, roll(got[tab[6, k], :, half], (16 * k - 16 * (r % 8)) % 128), acc)
        acc = jnp.where(wet[r:r + 1, :] > 0.0, acc, 0.0)
        for a in range(3):
            fine[pl.ds(3 * r + a, LEV, stride=LEV), :] = acc
    spread = spread_matrix((128, 384), False)
    stacked = jnp.concatenate([spread] * 3, axis=0)

    def level(l, carry):
        x = fine[pl.ds(pl.multiple_of(l * LEV, LEV), LEV), :]
        high = x.astype(jnp.bfloat16)
        rest = x - high.astype(jnp.float32)
        mid = rest.astype(jnp.bfloat16)
        low = (rest - mid.astype(jnp.float32)).astype(jnp.bfloat16)
        wide = jnp.dot(jnp.concatenate([high, mid, low], axis=1), stacked,
                       preferred_element_type=jnp.float32)
        out[l] = (light[...] * wide).astype(jnp.bfloat16)
        return carry

    lax.fori_loop(0, LEV, level, 0)


def heat(tab, got, wet, light):
    return pl.pallas_call(
        heat_kernel,
        in_specs=[pl.BlockSpec(memory_space=pltpu.SMEM)] + [pl.BlockSpec(memory_space=VM)] * 3,
        out_specs=pl.BlockSpec(memory_space=VM),
        out_shape=jax.ShapeDtypeStruct((LEV, 48, 384), jnp.bfloat16),
        scratch_shapes=[VM((LEV * LEV, 128), jnp.float32)],
        cost_estimate=pl.CostEstimate(flops=10**9, bytes_accessed=3 * 10**6, transcendentals=0),
        name="heat",
    )(tab, got, wet, light)


def tables(band, lat, lon):
    wet = band >= 0
    owner = band // SLOTS % 16
    tile = jnp.arange(128) // TILE
    slot_code = (lat * 16 + lon) * SLOTS + jnp.arange(SLOTS)
    hit = band[None, :] == slot_code[:, None]
    full = jnp.any(hit, axis=1)
    block = jnp.sum(jnp.where(hit, jnp.arange(128)[None, :], 0), axis=1)
    west = jnp.sum(jnp.where(jnp.roll(hit, -1, axis=1), band[None, :], 0), axis=1)
    east = jnp.sum(jnp.where(jnp.roll(hit, 1, axis=1), band[None, :], 0), axis=1)
    src = jnp.where(full, block // TILE, 0)
    used = jnp.any((src[None, :] == jnp.arange(16)[:, None]) & full[None, :], axis=1)
    spare = jnp.argmin(used).astype(jnp.int32)
    w_slot = jnp.where(full & (west >= 0), west % SLOTS, 0)
    e_slot = jnp.where(full & (east >= 0), east % SLOTS, 0)
    mine = lax.dynamic_slice_in_dim(band, lon * TILE, TILE)
    t_wet = mine >= 0
    t_own = mine // SLOTS % 16
    t_used = jnp.any((t_own[None, :] == jnp.arange(16)[:, None]) & t_wet[None, :], axis=1)
    t_spare = jnp.argmin(t_used).astype(jnp.int32)
    rows = [src, full, w_slot, e_slot, jnp.where(full, src, spare), t_wet, jnp.where(t_wet, t_own, t_spare), src]
    return jnp.stack([r.astype(jnp.int32) for r in rows])


def shift(x, axis, by, closed=True):
    n = lax.axis_size(axis)
    return lax.ppermute(x, axis, [(i, (i + by) % n) for i in range(n) if closed or 0 <= i + by < n])


def swap(x):
    return lax.all_to_all(x, "lon", split_axis=0, concat_axis=0, tiled=True)


def on_device(tracers, phys_fine, mix_coarse, surf_light, land_mask, owner_map):
    tab = tables(owner_map[0], lax.axis_index("lat"), lax.axis_index("lon"))
    wet = land_mask.astype(jnp.float32)
    wet_s = shift(wet[-1], "lat", 1, False)
    wet_n = shift(wet[0], "lat", -1, False)
    wet_w = shift(wet[:, -1], "lon", 1)
    wet_e = shift(wet[:, 0], "lon", -1)
    rows_out, w_out, e_out = pack(tab, tracers)
    open_e = wet * jnp.concatenate([wet[:, 1:], wet_e[:, None]], axis=1)
    open_w = wet * jnp.concatenate([wet_w[:, None], wet[:, :-1]], axis=1)
    open_n = wet * jnp.concatenate([wet[1:], wet_n[None]], axis=0)
    open_s = wet * jnp.concatenate([wet_s[None], wet[:-1]], axis=0)
    light = jnp.dot(surf_light, spread_matrix((384, 128), True, jnp.float32),
                    precision=lax.Precision.HIGHEST).reshape(SIDE, 3, 128)
    light = (light[:, 0] + light[:, 1] + light[:, 2]) / 9.0
    blank = jnp.zeros_like(wet)
    flags = jnp.stack([open_w, open_e, open_s, open_n, light, wet, blank, blank], axis=1)
    y, col = coarse(jnp.swapaxes(phys_fine, 1, 2), jnp.swapaxes(mix_coarse, 1, 2), flags)
    col = shift(col, "lon", 1)
    row = shift(y[SIDE - 1, 48:96], "lat", 1)
    phys = swap(package(tab, y, col, row))
    current = tracers
    for n in range(2):
        south, north = unpick(tab, swap(rows_out))
        rows = swap(repick(tab, shift(north, "lat", 1), shift(south, "lat", -1)))
        came_west = shift(e_out, "lon", 1)
        came_east = shift(w_out, "lon", -1)
        if n == 0:
            current, rows_out, w_out, e_out = step(False, tab, current, phys, rows, came_west, came_east)
        else:
            current, light_part = step(True, tab, current, phys, rows, came_west, came_east)
    return current, heat(tab, swap(light_part), wet, surf_light)


def solution(mesh):
    in_specs = (
        P(("lat", "lon"), None, None),
        P("lat", "lon", None),
        P("lat", "lon", None),
        P("lat", "lon"),
        P("lat", "lon"),
        P("lat", None),
    )
    out_specs = (P(("lat", "lon"), None, None), P(None, "lat", "lon"))
    return jax.shard_map(
        on_device, mesh=mesh, in_specs=in_specs, out_specs=out_specs, check_vma=False
    )
```

time: 1090 us -> 418 us (0.38)
  the two profiles are of different devices: /device:TPU:2 before, /device:TPU:4 now
where the time goes in v1:
time: 418 us; the launch traced here: 410 us
  waiting for transfers between devices  144 us (34%)
  Pallas kernels  141 us (34%)
  blocking collectives  53.6 us (13%)
  starting transfers between devices  52.6 us (13%)
  local copies, waits for them, and re-layouts  12.1 us (3%)
  other arithmetic  5.4 us (1%)
    ppermute x14, waiting for transfers between devices, shift(): lax.ppermute(x, axis, [(i, (i + by) % n) for i in range(n) if closed or 0...  118 us
    pallas_call x2, Pallas kernels, step(): pl.pallas_call(last_kernel if last else first_kernel, grid_spec=pltpu.Pre...  72.2 us
    all_to_all x2, blocking collectives, swap(): return lax.all_to_all(x, 'lon', split_axis=0, concat_axis=0, tiled=True)  53.6 us
    all_to_all x4, starting transfers between devices, swap(): return lax.all_to_all(x, 'lon', split_axis=0, concat_axis=0, tiled=True)  28.6 us
    all_to_all x4, waiting for transfers between devices, swap(): return lax.all_to_all(x, 'lon', split_axis=0, concat_axis=0, tiled=True)  26.3 us
    ppermute x14, starting transfers between devices, shift(): lax.ppermute(x, axis, [(i, (i + by) % n) for i in range(n) if closed or 0...  24 us
    pallas_call x1, Pallas kernels, pack(): pl.pallas_call(pack_kernel, grid_spec=pltpu.PrefetchScalarGridSpec(num_sc...  12.7 us
    pallas_call x1, Pallas kernels, coarse(): pl.pallas_call(coarse_kernel, grid=(SIDE,), in_specs=[pl.BlockSpec((3, 14...  12.2 us
  transfers between devices with their start and end apart: 18, of which 9 were waited for; matrix products, arithmetic and copies ran while one was open for 1% of the time, Pallas kernels for 8%

profile of v1, /device:TPU:4, one launch (start us, length us, event | category | flops | bytes accessed | tf_op | source)
XLA Modules:
  0.0 410.2 jit_solution(423867383863462524)
XLA Ops:
  6.7 12.7 %pack.1 = (f32[16,2,144,128]{3,2,1,0:T(8,128)}, f32[4,144,256]{2,1,0:T(8,128)}, f32[4,144,256]{2,1,0:T(8,128)}) custom-call(s32[8,8]{1,0:T(8,128)} %stack.16.tab, f32[8,1152,256]{2,1,0:T(8,128)} %c_ref.3), custom_call_target="tpu_custom_call" | custom-call | flops 10000000 | bytes 12000000 | tf_op jit(solution)/shard_map/pack/pallas_call | solution.py:76
  19.5 8.2 %all-to-all-start.1 = ((f32[16,2,144,128]{3,2,1,0:T(8,128)}), f32[16,2,144,128]{3,2,1,0:T(8,128)S(1)}, u32[]{:S(2)}, u32[]{:S(2)}) async-start(f32[16,2,144,128]{3,2,1,0:T(8,128)} %get-tuple-element.23), calls=%async_computation.1 | async-start | bytes 4718592 | tf_op jit(solution)/shard_map/all_to_all | solution.py:557
  32.2 5.3 %collective-permute-start.1 = (f32[16]{0:T(128)S(1)}, f32[16]{0:T(128)S(1)}, u32[]{:S(2)}, u32[]{:S(2)}) collective-permute-start(f32[16]{0:T(128)S(1)} %get-tuple-element.36), channel_id=1, source_target_pairs={{0,15},{1,0},{2,1},{3,2},{4,3},{5,4},{6,5},{7,6},{8,7},{9,8},{10,9... | collective-permute-start | bytes 200 | tf_op jit(solution)/shard_map/ppermute | solution.py:553
  38.1 15.7 %collective-permute-done.1 = f32[16]{0:T(128)S(1)} collective-permute-done((f32[16]{0:T(128)S(1)}, f32[16]{0:T(128)S(1)}, u32[]{:S(2)}, u32[]{:S(2)}) %collective-permute-start.1) | collective-permute-done | bytes 96 | tf_op jit(solution)/shard_map/ppermute | solution.py:553
  53.9 6.0 %collective-permute-done = f32[16]{0:T(128)S(1)} collective-permute-done((f32[16]{0:T(128)S(1)}, f32[16]{0:T(128)S(1)}, u32[]{:S(2)}, u32[]{:S(2)}) %collective-permute-start) | collective-permute-done | bytes 96 | tf_op jit(solution)/shard_map/ppermute | solution.py:553
  60.8 12.2 %coarse.1 = (f32[16,200,128]{2,1,0:T(8,128)}, f32[48,128]{1,0:T(8,128)}) custom-call(bf16[48,144,384]{2,1,0:T(8,128)(2,1)} %bitcast.63, bf16[16,48,128]{2,1,0:T(8,128)(2,1)} %bitcast.65, f32[16,8,128]{2,1,0:T(8,128)} %stack.40.flags), custom_call_target="tpu_custom_call" | custom-call | flops 1000000000 | bytes 8000000 | tf_op jit(solution)/shard_map/coarse/pallas_call | solution.py:382
  77.0 4.1 %collective-permute-done.4.col_ref = f32[48,128]{1,0:T(8,128)S(1)} collective-permute-done((f32[48,128]{1,0:T(8,128)}, f32[48,128]{1,0:T(8,128)S(1)}, u32[]{:S(2)}, u32[]{:S(2)}) %collective-permute-start.4) | collective-permute-done | bytes 24608 | tf_op jit(solution)/shard_map/ppermute | solution.py:553
  81.7 8.0 %package.1 = f32[16,224,256]{2,1,0:T(8,128)} custom-call(s32[8,8]{1,0:T(8,128)} %stack.16.tab, f32[16,200,128]{2,1,0:T(8,128)} %get-tuple-element.21.y_ref, f32[48,128]{1,0:T(8,128)} %copy-done.14, f32[48,128]{1,0:T(8,128)} %copy-done.13), custom_call_target="tpu_custom_call" | custom-call | flops 10000000 | bytes 4000000 | tf_op jit(solution)/shard_map/package/pallas_call | solution.py:426
  91.1 4.5 %all-to-all-start = ((f32[16,224,256]{2,1,0:T(8,128)}), f32[16,224,256]{2,1,0:T(8,128)}, u32[]{:S(2)}, u32[]{:S(2)}) async-start(f32[16,224,256]{2,1,0:T(8,128)} %package.1), calls=%async_computation | async-start | bytes 7340032 | tf_op jit(solution)/shard_map/all_to_all | solution.py:557
  95.6 6.0 %unpick.2 = (f32[8,144,128]{2,1,0:T(8,128)}, f32[8,144,128]{2,1,0:T(8,128)}) custom-call(s32[8,8]{1,0:T(8,128)} %stack.16.tab, f32[16,2,144,128]{3,2,1,0:T(8,128)} %copy-done.2), custom_call_target="tpu_custom_call" | custom-call | flops 1000000 | bytes 2400000 | tf_op jit(solution)/shard_map/unpick/pallas_call | solution.py:452
  103.4 7.8 %collective-permute-done.6.south = f32[8,144,128]{2,1,0:T(8,128)S(1)} collective-permute-done((f32[8,144,128]{2,1,0:T(8,128)}, f32[8,144,128]{2,1,0:T(8,128)S(1)}, u32[]{:S(2)}, u32[]{:S(2)}) %collective-permute-start.6) | collective-permute-done | bytes 589856 | tf_op jit(solution)/shard_map/ppermute | solution.py:553
  112.8 6.0 %repick.2 = f32[16,2,144,128]{3,2,1,0:T(8,128)} custom-call(s32[8,8]{1,0:T(8,128)} %stack.16.tab, f32[8,144,128]{2,1,0:T(8,128)} %copy-done.7, f32[8,144,128]{2,1,0:T(8,128)} %copy-done.9), custom_call_target="tpu_custom_call" | custom-call | flops 1000000 | bytes 2400000 | tf_op jit(solution)/shard_map/repick/pallas_call | solution.py:473
  118.8 26.3 %all-to-all-done.phys = f32[16,224,256]{2,1,0:T(8,128)} async-done(((f32[16,224,256]{2,1,0:T(8,128)}), f32[16,224,256]{2,1,0:T(8,128)}, u32[]{:S(2)}, u32[]{:S(2)}) %all-to-all-start) | async-done | bytes 3670048 | tf_op jit(solution)/shard_map/all_to_all | solution.py:557
  145.1 12.2 %all-to-all-start.2 = ((f32[16,2,144,128]{3,2,1,0:T(8,128)}), f32[16,2,144,128]{3,2,1,0:T(8,128)S(1)}, u32[]{:S(2)}, u32[]{:S(2)}) async-start(f32[16,2,144,128]{3,2,1,0:T(8,128)} %repick.2), calls=%async_computation.2 | async-start | bytes 4718592 | tf_op jit(solution)/shard_map/all_to_all | solution.py:557
  162.7 38.2 %collective-permute-done.8.west = f32[4,144,256]{2,1,0:T(8,128)S(1)} collective-permute-done((f32[4,144,256]{2,1,0:T(8,128)}, f32[4,144,256]{2,1,0:T(8,128)S(1)}, u32[]{:S(2)}, u32[]{:S(2)}) %collective-permute-start.8) | collective-permute-done | bytes 589856 | tf_op jit(solution)/shard_map/ppermute | solution.py:553
  203.3 39.9 %first_step.1 = (f32[8,1152,256]{2,1,0:T(8,128)}, f32[16,2,144,128]{3,2,1,0:T(8,128)}, f32[4,144,256]{2,1,0:T(8,128)}, f32[4,144,256]{2,1,0:T(8,128)}) custom-call(s32[8,8]{1,0:T(8,128)} %stack.16.tab, f32[8,1152,256]{2,1,0:T(8,128)} %c_ref.3, f32[16,224,256]{2,1,0:T(8,128)} %all-to-all-done.phys, f32[16,2,144,128]{3,2,1,0:T(8,128)} %copy-done, ...), custom_call_target="tpu_custom_call" | custom-call | flops 100000000 | bytes 25000000 | tf_op jit(solution)/shard_map/first_step/pallas_call | solution.py:327
  243.2 34.6 %all_to_all.30.got = f32[16,2,144,128]{3,2,1,0:T(8,128)} all-to-all(f32[16,2,144,128]{3,2,1,0:T(8,128)} %get-tuple-element.29), channel_id=1, replica_groups=mesh['lat'=8,'lon'=16] {'lon'}, dimensions={0} | all-to-all | bytes 4718592 | tf_op jit(solution)/shard_map/all_to_all | solution.py:557
  277.9 6.0 %unpick.3 = (f32[8,144,128]{2,1,0:T(8,128)}, f32[8,144,128]{2,1,0:T(8,128)}) custom-call(s32[8,8]{1,0:T(8,128)} %stack.16.tab, f32[16,2,144,128]{3,2,1,0:T(8,128)} %all_to_all.30.got), custom_call_target="tpu_custom_call" | custom-call | flops 1000000 | bytes 2400000 | tf_op jit(solution)/shard_map/unpick/pallas_call | solution.py:452
  285.6 7.8 %collective-permute-done.10.south = f32[8,144,128]{2,1,0:T(8,128)S(1)} collective-permute-done((f32[8,144,128]{2,1,0:T(8,128)}, f32[8,144,128]{2,1,0:T(8,128)S(1)}, u32[]{:S(2)}, u32[]{:S(2)}) %collective-permute-start.10) | collective-permute-done | bytes 589856 | tf_op jit(solution)/shard_map/ppermute | solution.py:553
  295.1 6.0 %repick.3 = f32[16,2,144,128]{3,2,1,0:T(8,128)} custom-call(s32[8,8]{1,0:T(8,128)} %stack.16.tab, f32[8,144,128]{2,1,0:T(8,128)} %copy-done.8, f32[8,144,128]{2,1,0:T(8,128)} %copy-done.10), custom_call_target="tpu_custom_call" | custom-call | flops 1000000 | bytes 2400000 | tf_op jit(solution)/shard_map/repick/pallas_call | solution.py:473
  310.2 35.2 %collective-permute-done.12.west = f32[4,144,256]{2,1,0:T(8,128)S(1)} collective-permute-done((f32[4,144,256]{2,1,0:T(8,128)}, f32[4,144,256]{2,1,0:T(8,128)S(1)}, u32[]{:S(2)}, u32[]{:S(2)}) %collective-permute-start.12) | collective-permute-done | bytes 589856 | tf_op jit(solution)/shard_map/ppermute | solution.py:553
  347.2 32.3 %last_step.1 = (f32[8,1152,256]{2,1,0:T(8,128)}, f32[16,48,256]{2,1,0:T(8,128)}) custom-call(s32[8,8]{1,0:T(8,128)} %stack.16.tab, f32[8,1152,256]{2,1,0:T(8,128)} %get-tuple-element.28.c_ref, f32[16,224,256]{2,1,0:T(8,128)} %all-to-all-done.phys, f32[16,2,144,128]{3,2,1,0:T(8,128)} %copy-done.1, f32[4,144,256]{2,1,0:T(8,128)} %copy-done.4, ...), custom_call_target="tpu_custom_call" | custom-call | flops 100000000 | bytes 25000000 | tf_op jit(solution)/shard_map/last_step/pallas_call | solution.py:327
  379.5 19.0 %all_to_all.31.got = f32[16,48,256]{2,1,0:T(8,128)} all-to-all(f32[16,48,256]{2,1,0:T(8,128)} %get-tuple-element.35), channel_id=1, replica_groups=mesh['lat'=8,'lon'=16] {'lon'}, dimensions={0} | all-to-all | bytes 1572864 | tf_op jit(solution)/shard_map/all_to_all | solution.py:557
  398.5 11.7 %heat.1 = bf16[48,48,384]{2,1,0:T(8,128)(2,1)} custom-call(s32[8,8]{1,0:T(8,128)} %stack.16.tab, f32[16,48,256]{2,1,0:T(8,128)} %all_to_all.31.got, f32[16,128]{1,0:T(8,128)} %copy-done.11, f32[48,384]{1,0:T(8,128)} %light.1), custom_call_target="tpu_custom_call" | custom-call | flops 1000000000 | bytes 3000000 | tf_op jit(solution)/shard_map/heat/pallas_call | solution.py:516
  (89 shorter events, 43.6 us)
Async XLA Ops:
  19.5 8.2 %copy-start.12 = (s32[16,128]{1,0:T(8,128)S(1)}, s32[16,128]{1,0:T(8,128)}, u32[]{:S(2)}) copy-start(s32[16,128]{1,0:T(8,128)} %param.10) | copy-start | bytes 24580
  19.5 18.1 %copy-start.15 = (f32[48,384]{1,0:T(8,128)S(1)}, f32[48,384]{1,0:T(8,128)}, u32[]{:S(2)}) copy-start(f32[48,384]{1,0:T(8,128)} %light.1) | copy-start | bytes 221188
  19.5 70.2 %all-to-all-start.1 = ((f32[16,2,144,128]{3,2,1,0:T(8,128)}), f32[16,2,144,128]{3,2,1,0:T(8,128)S(1)}, u32[]{:S(2)}, u32[]{:S(2)}) async-start(f32[16,2,144,128]{3,2,1,0:T(8,128)} %get-tuple-element.23), calls=%async_computation.1 | async-start | bytes 4718592 | tf_op jit(solution)/shard_map/all_to_all | solution.py:557
  27.7 45.3 %copy-start.11 = (f32[16,128]{1,0:T(8,128)}, f32[16,128]{1,0:T(8,128)S(1)}, u32[]{:S(2)}) copy-start(f32[16,128]{1,0:T(8,128)S(1)} %convert_element_type.20.wet) | copy-start | bytes 24580
  27.7 32.3 %collective-permute-start.3 = (f32[128]{0:T(128)S(1)}, f32[128]{0:T(128)S(1)}, u32[]{:S(2)}, u32[]{:S(2)}) collective-permute-start(f32[128]{0:T(128)S(1)} %get-tuple-element.49), channel_id=1, source_target_pairs={{16,0},{32,16},{48,32},{64,48},{80,64},{96,80},{112,96},{17,1},{33... | collective-permute-start | bytes 1544 | tf_op jit(solution)/shard_map/ppermute | solution.py:553
  29.7 30.3 %collective-permute-start.2 = (f32[128]{0:T(128)S(1)}, f32[128]{0:T(128)S(1)}, u32[]{:S(2)}, u32[]{:S(2)}) collective-permute-start(f32[128]{0:T(128)S(1)} %get-tuple-element.50), channel_id=1, source_target_pairs={{0,16},{16,32},{32,48},{48,64},{64,80},{80,96},{96,112},{1,17},{17... | collective-permute-start | bytes 1544 | tf_op jit(solution)/shard_map/ppermute | solution.py:553
  32.2 21.5 %collective-permute-start.1 = (f32[16]{0:T(128)S(1)}, f32[16]{0:T(128)S(1)}, u32[]{:S(2)}, u32[]{:S(2)}) collective-permute-start(f32[16]{0:T(128)S(1)} %get-tuple-element.36), channel_id=1, source_target_pairs={{0,15},{1,0},{2,1},{3,2},{4,3},{5,4},{6,5},{7,6},{8,7},{9,8},{10,9... | collective-permute-start | bytes 200 | tf_op jit(solution)/shard_map/ppermute | solution.py:553
  37.6 22.3 %collective-permute-start = (f32[16]{0:T(128)S(1)}, f32[16]{0:T(128)S(1)}, u32[]{:S(2)}, u32[]{:S(2)}) collective-permute-start(f32[16]{0:T(128)S(1)} %get-tuple-element.37), channel_id=1, source_target_pairs={{0,1},{1,2},{2,3},{3,4},{4,5},{5,6},{6,7},{7,8},{8,9},{9,10},{10,1... | collective-permute-start | bytes 200 | tf_op jit(solution)/shard_map/ppermute | solution.py:553
  73.8 3.3 collective-permute-start.5
  73.8 7.4 %collective-permute-start.4 = (f32[48,128]{1,0:T(8,128)}, f32[48,128]{1,0:T(8,128)S(1)}, u32[]{:S(2)}, u32[]{:S(2)}) collective-permute-start(f32[48,128]{1,0:T(8,128)} %get-tuple-element.22), channel_id=1, source_target_pairs={{0,1},{1,2},{2,3},{3,4},{4,5},{5,6},{6,7},{7,8},{8,9},{9,10},{10,1... | collective-permute-start | bytes 73736 | tf_op jit(solution)/shard_map/ppermute | solution.py:553
  77.0 4.1 %copy-start.13 = (f32[48,128]{1,0:T(8,128)}, f32[48,128]{1,0:T(8,128)S(1)}, u32[]{:S(2)}) copy-start(f32[48,128]{1,0:T(8,128)S(1)} %collective-permute-done.5.row_ref) | copy-start | bytes 73732
  89.7 1.4 copy-start.2
  91.1 54.0 %all-to-all-start = ((f32[16,224,256]{2,1,0:T(8,128)}), f32[16,224,256]{2,1,0:T(8,128)}, u32[]{:S(2)}, u32[]{:S(2)}) async-start(f32[16,224,256]{2,1,0:T(8,128)} %package.1), calls=%async_computation | async-start | bytes 7340032 | tf_op jit(solution)/shard_map/all_to_all | solution.py:557
  101.6 9.5 %collective-permute-start.6 = (f32[8,144,128]{2,1,0:T(8,128)}, f32[8,144,128]{2,1,0:T(8,128)S(1)}, u32[]{:S(2)}, u32[]{:S(2)}) collective-permute-start(f32[8,144,128]{2,1,0:T(8,128)} %get-tuple-element.24), channel_id=1, source_target_pairs={{0,16},{16,32},{32,48},{48,64},{64,80},{80,96},{96,112},{112,0},{1... | collective-permute-start | bytes 1769480 | tf_op jit(solution)/shard_map/ppermute | solution.py:553
  101.8 9.3 %collective-permute-start.7 = (f32[8,144,128]{2,1,0:T(8,128)}, f32[8,144,128]{2,1,0:T(8,128)S(1)}, u32[]{:S(2)}, u32[]{:S(2)}) collective-permute-start(f32[8,144,128]{2,1,0:T(8,128)} %get-tuple-element.25), channel_id=1, source_target_pairs={{0,112},{16,0},{32,16},{48,32},{64,48},{80,64},{96,80},{112,96},{1... | collective-permute-start | bytes 1769480 | tf_op jit(solution)/shard_map/ppermute | solution.py:553
  145.1 55.9 %all-to-all-start.2 = ((f32[16,2,144,128]{3,2,1,0:T(8,128)}), f32[16,2,144,128]{3,2,1,0:T(8,128)S(1)}, u32[]{:S(2)}, u32[]{:S(2)}) async-start(f32[16,2,144,128]{3,2,1,0:T(8,128)} %repick.2), calls=%async_computation.2 | async-start | bytes 4718592 | tf_op jit(solution)/shard_map/all_to_all | solution.py:557
  157.3 43.6 %collective-permute-start.8 = (f32[4,144,256]{2,1,0:T(8,128)}, f32[4,144,256]{2,1,0:T(8,128)S(1)}, u32[]{:S(2)}, u32[]{:S(2)}) collective-permute-start(f32[4,144,256]{2,1,0:T(8,128)} %get-tuple-element.26), channel_id=1, source_target_pairs={{0,1},{1,2},{2,3},{3,4},{4,5},{5,6},{6,7},{7,8},{8,9},{9,10},{10,1... | collective-permute-start | bytes 1769480 | tf_op jit(solution)/shard_map/ppermute | solution.py:553
  159.2 41.7 %collective-permute-start.9 = (f32[4,144,256]{2,1,0:T(8,128)}, f32[4,144,256]{2,1,0:T(8,128)S(1)}, u32[]{:S(2)}, u32[]{:S(2)}) collective-permute-start(f32[4,144,256]{2,1,0:T(8,128)} %get-tuple-element.27), channel_id=1, source_target_pairs={{0,15},{1,0},{2,1},{3,2},{4,3},{5,4},{6,5},{7,6},{8,7},{9,8},{10,9... | collective-permute-start | bytes 1769480 | tf_op jit(solution)/shard_map/ppermute | solution.py:553
  283.9 9.5 %collective-permute-start.10 = (f32[8,144,128]{2,1,0:T(8,128)}, f32[8,144,128]{2,1,0:T(8,128)S(1)}, u32[]{:S(2)}, u32[]{:S(2)}) collective-permute-start(f32[8,144,128]{2,1,0:T(8,128)} %get-tuple-element.30), channel_id=1, source_target_pairs={{0,16},{16,32},{32,48},{48,64},{64,80},{80,96},{96,112},{112,0},{1... | collective-permute-start | bytes 1769480 | tf_op jit(solution)/shard_map/ppermute | solution.py:553
  283.9 9.5 %collective-permute-start.11 = (f32[8,144,128]{2,1,0:T(8,128)}, f32[8,144,128]{2,1,0:T(8,128)S(1)}, u32[]{:S(2)}, u32[]{:S(2)}) collective-permute-start(f32[8,144,128]{2,1,0:T(8,128)} %get-tuple-element.31), channel_id=1, source_target_pairs={{0,112},{16,0},{32,16},{48,32},{64,48},{80,64},{96,80},{112,96},{1... | collective-permute-start | bytes 1769480 | tf_op jit(solution)/shard_map/ppermute | solution.py:553
  301.1 44.4 %all-to-all-start.4 = ((f32[16,2,144,128]{3,2,1,0:T(8,128)}), f32[16,2,144,128]{3,2,1,0:T(8,128)S(1)}, u32[]{:S(2)}, u32[]{:S(2)}) async-start(f32[16,2,144,128]{3,2,1,0:T(8,128)} %repick.3), calls=%async_computation.4 | async-start | bytes 4718592 | tf_op jit(solution)/shard_map/all_to_all | solution.py:557
  304.8 40.7 %collective-permute-start.12 = (f32[4,144,256]{2,1,0:T(8,128)}, f32[4,144,256]{2,1,0:T(8,128)S(1)}, u32[]{:S(2)}, u32[]{:S(2)}) collective-permute-start(f32[4,144,256]{2,1,0:T(8,128)} %get-tuple-element.32), channel_id=1, source_target_pairs={{0,1},{1,2},{2,3},{3,4},{4,5},{5,6},{6,7},{7,8},{8,9},{9,10},{10,1... | collective-permute-start | bytes 1769480 | tf_op jit(solution)/shard_map/ppermute | solution.py:553
  306.7 38.8 %collective-permute-start.13 = (f32[4,144,256]{2,1,0:T(8,128)}, f32[4,144,256]{2,1,0:T(8,128)S(1)}, u32[]{:S(2)}, u32[]{:S(2)}) collective-permute-start(f32[4,144,256]{2,1,0:T(8,128)} %get-tuple-element.33), channel_id=1, source_target_pairs={{0,15},{1,0},{2,1},{3,2},{4,3},{5,4},{6,5},{7,6},{8,7},{9,8},{10,9... | collective-permute-start | bytes 1769480 | tf_op jit(solution)/shard_map/ppermute | solution.py:553
  345.5 1.7 copy-start.1
  (10 other events, 9.0 us)

commit v2 on v1

--- a/solution.py
+++ b/solution.py
@@ -17,6 +17,7 @@
 DIFF = 0.08
 VM = pltpu.VMEM
 ROWS3 = 3 * LEV
+HALF = ROWS3 // 2
 
 
 def pos(v):
@@ -35,28 +36,42 @@
     lane = lanes()
     group = lane // SIDE
     col = lane % SIDE
-    base = odd * 8
+    even = lane % 2 == 0
+    low = lane < SIDE
     for m in range(3):
         blank = jnp.zeros((LEV, 128), jnp.float32)
-        south, north = blank, blank
-        west, east = [blank, blank], [blank, blank]
+        ends = [blank, blank]
+        both = [blank, blank]
         for g in range(8):
             t = 3 * g + m
             a = c_ref[0, t * LEV:(t + 1) * LEV, 0:128]
             b = c_ref[0, t * LEV:(t + 1) * LEV, 128:256]
-            south = jnp.where(group == g, roll(a, 16 * g) if g else a, south)
-            north = jnp.where(group == g, roll(b, (16 * g + 16) % 128), north)
+            end = jnp.where(low, a, b)
+            ends[g % 2] = jnp.where((group == g) | (group == (g + 7) % 8), roll(end, 16 * g) if g else end, ends[g % 2])
+            here = (col == 2 * g) | (col == (2 * g + 15) % 16)
             for h, v in enumerate((a, b)):
-                west[h] = jnp.where(col == g, roll(v, g) if g else v, west[h])
-                east[h] = jnp.where(col == g, roll(v, (g - 15) % 128), east[h])
+                both[h] = jnp.where(here, roll(v, 2 * g) if g else v, both[h])
+        flat = group % 2 == 0
+        put_rows(rows_ref, 0, m, jnp.where(flat, ends[0], ends[1]))
+        put_rows(rows_ref, 1, m, jnp.where(flat, ends[1], ends[0]))
         at = slice(m * LEV, (m + 1) * LEV)
-        rows_ref[0, 0, at, :] = south
-        rows_ref[0, 1, at, :] = north
-        mine = (col // 8) == odd
+        mine = (lane % 2) == odd
         for h in range(2):
             hs = slice(h * 128, (h + 1) * 128)
-            w_ref[0, at, hs] = jnp.where(mine, roll(west[h], base), w_ref[0, at, hs])
-            e_ref[0, at, hs] = jnp.where(mine, roll(east[h], base), e_ref[0, at, hs])
+            turned = roll(both[h], odd)
+            w_ref[0, at, hs] = jnp.where(mine, turned, w_ref[0, at, hs])
+            e_ref[0, at, hs] = jnp.where(mine, e_ref[0, at, hs], turned)
+
+
+def put_rows(rows_ref, d, m, x):
+    lo = m * LEV
+    if lo < HALF:
+        n = min(LEV, HALF - lo)
+        rows_ref[0, 0, d, lo:lo + n, :] = x[:n]
+        if n < LEV:
+            rows_ref[0, 1, d, 0:LEV - n, :] = x[n:]
+    else:
+        rows_ref[0, 1, d, lo - HALF:lo - HALF + LEV, :] = x
 
 
 def clear_first(odd, *refs):
@@ -80,13 +95,13 @@
             grid=(SLOTS,),
             in_specs=[pl.BlockSpec((1, NTR * LEV, CELLS), lambda j, tab: (j, 0, 0))],
             out_specs=[
-                pl.BlockSpec((1, 2, ROWS3, 128), lambda j, tab: (tab[4, j], 0, 0, 0)),
+                pl.BlockSpec((1, 2, 2, HALF, 128), lambda j, tab: (tab[8, j], 0, 0, 0, 0)),
                 pl.BlockSpec((1, ROWS3, CELLS), lambda j, tab: (j // 2, 0, 0)),
                 pl.BlockSpec((1, ROWS3, CELLS), lambda j, tab: (j // 2, 0, 0)),
             ],
         ),
         out_shape=[
-            jax.ShapeDtypeStruct((16, 2, ROWS3, 128), jnp.float32),
+            jax.ShapeDtypeStruct((8, 2, 2, HALF, 128), jnp.float32),
             jax.ShapeDtypeStruct((4, ROWS3, CELLS), jnp.float32),
             jax.ShapeDtypeStruct((4, ROWS3, CELLS), jnp.float32),
         ],
@@ -191,7 +206,7 @@
                    preferred_element_type=jnp.float32)
 
 
-def slot_step(tab, c_ref, phys, rows, west, east, out, coef, par_ref):
+def slot_step(tab, c_ref, phys, rows, west, east, out, coef, par_ref, cross, along):
     j = pl.program_id(0)
     w_odd = tab[2, j] % 2
     e_odd = tab[3, j] % 2
@@ -235,23 +250,33 @@
         flux = k * (pltpu.roll(moved, LEV - 1, 0) - moved)
         return moved + flux - pltpu.roll(flux, 1, 0)
 
+    wide = lax.broadcasted_iota(jnp.int32, (HALF, 128), 1)
+    flat = (wide // SIDE) % 2 == 0
+    for p in range(2):
+        hp = slice(p * HALF, (p + 1) * HALF)
+        upper = rows[0, p, 1, :, :]
+        under = roll(rows[0, p, 0, :, :], 32)
+        cross[0, hp, :] = jnp.where(flat, upper, under)
+        cross[1, hp, :] = jnp.where(flat, under, upper)
+        for h in range(2):
+            along[hp, H[h]] = jnp.where(wide % 2 == 0, roll(west[0, hp, H[h]], 128 - 15 - w_odd),
+                                        roll(east[0, hp, H[h]], 15 - e_odd))
+
     def group(g, carry):
         for m in range(3):
             at = pl.ds(pl.multiple_of((3 * g + m) * LEV, LEV), LEV)
             hm = slice(m * LEV, (m + 1) * LEV)
             a = c_ref[0, at, H[0]]
             b = c_ref[0, at, H[1]]
-            hs = roll(rows[0, 0, hm, :], (128 - 16 * g) % 128)
-            hn = roll(rows[0, 1, hm, :], 112 - 16 * g)
+            ends = roll(cross[lax.rem(g, 2), hm, :], 112 - 16 * g)
             an, bn = roll(a, 112), roll(b, 112)
             as_, bs = roll(a, 16), roll(b, 16)
-            north = (jnp.where(high, bn, an), jnp.where(high, hn, bn))
-            south = (jnp.where(low, hs, as_), jnp.where(low, as_, bs))
-            w_shift = (128 - (8 * w_odd + g)) % 128
-            e_shift = 15 - (8 * e_odd + g)
+            north = (jnp.where(high, bn, an), jnp.where(high, ends, bn))
+            south = (jnp.where(low, ends, as_), jnp.where(low, as_, bs))
             for h, v in enumerate((a, b)):
-                vw = jnp.where(at_w, roll(west[0, hm, H[h]], w_shift), roll(v, 1))
-                ve = jnp.where(at_e, roll(east[0, hm, H[h]], e_shift), roll(v, 127))
+                sides = roll(along[hm, H[h]], lax.rem(128 - 2 * g, 128))
+                vw = jnp.where(at_w, sides, roll(v, 1))
+                ve = jnp.where(at_e, sides, roll(v, 127))
                 moved = (coef[0, :, H[h]] * v + coef[1, :, H[h]] * ve + coef[2, :, H[h]] * vw
                          + coef[3, :, H[h]] * north[h] + coef[4, :, H[h]] * south[h])
                 out[0, at, H[h]] = mix(moved, coef[5, :, H[h]])
@@ -283,13 +308,13 @@
         lax.fori_loop(0, LEV // 8, chunk, 0)
 
 
-def first_kernel(tab, c_ref, phys, rows, west, east, out, rows_out, w_out, e_out, coef, par_ref):
+def first_kernel(tab, c_ref, phys, rows, west, east, out, rows_out, w_out, e_out, coef, par_ref, cross, along):
     j = pl.program_id(0)
     odd = j % 2
 
     @pl.when(tab[1, j] == 1)
     def _():
-        slot_step(tab, c_ref, phys, rows, west, east, out, coef, par_ref)
+        slot_step(tab, c_ref, phys, rows, west, east, out, coef, par_ref, cross, along)
 
     @pl.when(tab[1, j] == 0)
     def _():
@@ -299,12 +324,12 @@
     pack_edges(out, rows_out, w_out, e_out, odd)
 
 
-def last_kernel(tab, c_ref, phys, rows, west, east, out, light_out, coef, par_ref):
+def last_kernel(tab, c_ref, phys, rows, west, east, out, light_out, coef, par_ref, cross, along):
     j = pl.program_id(0)
 
     @pl.when(tab[1, j] == 1)
     def _():
-        slot_step(tab, c_ref, phys, rows, west, east, out, coef, par_ref)
+        slot_step(tab, c_ref, phys, rows, west, east, out, coef, par_ref, cross, along)
         absorb = 0.04 + 0.02 * (pos(out[0, 480:528, :]) + pos(out[0, 528:576, :]))
         above = depth(absorb)
         light_out[0] = jnp.exp(-above) - jnp.exp(-(above + absorb))
@@ -322,8 +347,8 @@
         outs = [pl.BlockSpec((1, LEV, CELLS), lambda j, tab: (tab[4, j], 0, 0))]
         shapes = [jax.ShapeDtypeStruct((16, LEV, CELLS), jnp.float32)]
     else:
-        outs = [pl.BlockSpec((1, 2, ROWS3, 128), lambda j, tab: (tab[4, j], 0, 0, 0)), edge_spec, edge_spec]
-        shapes = [jax.ShapeDtypeStruct((16, 2, ROWS3, 128), jnp.float32), edge_shape, edge_shape]
+        outs = [pl.BlockSpec((1, 2, 2, HALF, 128), lambda j, tab: (tab[8, j], 0, 0, 0, 0)), edge_spec, edge_spec]
+        shapes = [jax.ShapeDtypeStruct((8, 2, 2, HALF, 128), jnp.float32), edge_shape, edge_shape]
     return pl.pallas_call(
         last_kernel if last else first_kernel,
         grid_spec=pltpu.PrefetchScalarGridSpec(
@@ -332,12 +357,13 @@
             in_specs=[
                 pl.BlockSpec((1, NTR * LEV, CELLS), lambda j, tab: (j, 0, 0)),
                 pl.BlockSpec((1, PHYS, CELLS), lambda j, tab: (tab[0, j], 0, 0)),
-                pl.BlockSpec((1, 2, ROWS3, 128), lambda j, tab: (tab[0, j], 0, 0, 0)),
+                pl.BlockSpec((1, 2, 2, HALF, 128), lambda j, tab: (tab[7, j], 0, 0, 0, 0)),
                 pl.BlockSpec((1, ROWS3, CELLS), lambda j, tab: (tab[2, j] // 2, 0, 0)),
                 pl.BlockSpec((1, ROWS3, CELLS), lambda j, tab: (tab[3, j] // 2, 0, 0)),
             ],
             out_specs=[pl.BlockSpec((1, NTR * LEV, CELLS), lambda j, tab: (j, 0, 0))] + outs,
-            scratch_shapes=[VM((6, LEV, CELLS), jnp.float32), VM((LEV, CELLS), jnp.float32)],
+            scratch_shapes=[VM((6, LEV, CELLS), jnp.float32), VM((LEV, CELLS), jnp.float32),
+                            VM((2, ROWS3, 128), jnp.float32), VM((ROWS3, CELLS), jnp.float32)],
         ),
         out_shape=[jax.ShapeDtypeStruct((SLOTS, NTR * LEV, CELLS), jnp.float32)] + shapes,
         cost_estimate=pl.CostEstimate(flops=10**8, bytes_accessed=25 * 10**6, transcendentals=10**6),
@@ -441,47 +467,113 @@
     )(tab, y, col, row)
 
 
-def unpick_kernel(tab, got, south, north):
-    wet = tab[5, pl.program_id(0)] == 1
-    south[0] = jnp.where(wet, got[0, 0], 0.0)
-    north[0] = jnp.where(wet, got[0, 1], 0.0)
-
-
-def unpick(tab, got):
-    one = pl.BlockSpec((1, ROWS3, 128), lambda k, tab: (k, 0, 0))
-    return pl.pallas_call(
-        unpick_kernel,
-        grid_spec=pltpu.PrefetchScalarGridSpec(
-            num_scalar_prefetch=1,
-            grid=(TILE,),
-            in_specs=[pl.BlockSpec((1, 2, ROWS3, 128), lambda k, tab: (tab[6, k], 0, 0, 0))],
-            out_specs=[one, one],
-        ),
-        out_shape=[jax.ShapeDtypeStruct((TILE, ROWS3, 128), jnp.float32)] * 2,
-        cost_estimate=pl.CostEstimate(flops=10**6, bytes_accessed=24 * 10**5, transcendentals=0),
-        name="unpick",
-    )(tab, got)
-
-
-def repick_kernel(tab, south, north, out):
-    out[0, 0] = south[0]
-    out[0, 1] = north[0]
-
-
-def repick(tab, south, north):
-    one = pl.BlockSpec((1, ROWS3, 128), lambda k, tab: (k, 0, 0))
-    return pl.pallas_call(
-        repick_kernel,
-        grid_spec=pltpu.PrefetchScalarGridSpec(
-            num_scalar_prefetch=1,
-            grid=(TILE,),
-            in_specs=[one, one],
-            out_specs=pl.BlockSpec((1, 2, ROWS3, 128), lambda k, tab: (tab[6, k], 0, 0, 0)),
-        ),
-        out_shape=jax.ShapeDtypeStruct((16, 2, ROWS3, 128), jnp.float32),
-        cost_estimate=pl.CostEstimate(flops=10**6, bytes_accessed=24 * 10**5, transcendentals=0),
-        name="repick",
-    )(tab, south, north)
+MESH = pl.DeviceIdType.MESH
+
+
+def halo_kernel(tab, up_ref, w_ref, e_ref, rows_ref, from_w, from_e, got_s, got_n, pick,
+                up_send, up_recv, dn_send, dn_recv, we_send, we_recv):
+    lat, lon = lax.axis_index("lat"), lax.axis_index("lon")
+    bands, count = lax.axis_size("lat"), lax.axis_size("lon")
+    sides = (lax.rem(lat + 1, bands), lax.rem(lat + bands - 1, bands))
+    got = (got_s, got_n)
+    barrier = pltpu.get_barrier_semaphore()
+
+    def greet(d, carry):
+        peer = lax.rem(lon + d, count)
+        for side in sides:
+            pl.semaphore_signal(barrier, inc=1, device_id=(side, peer), device_id_type=MESH)
+        return carry
+
+    def greet_band(d, carry):
+        pl.semaphore_signal(barrier, inc=1, device_id=(lat, lax.rem(lon + d, count)), device_id_type=MESH)
+        return carry
+
+    lax.fori_loop(0, count, greet, 0)
+    lax.fori_loop(1, count, greet_band, 0)
+    pl.semaphore_wait(barrier, 3 * count - 1)
+
+    def up(n, d):
+        peer = lax.rem(lon + d, count)
+        return pltpu.make_async_remote_copy(
+            src_ref=up_ref.at[peer, 1 - n], dst_ref=got[n].at[lon],
+            send_sem=up_send.at[n, d], recv_sem=up_recv.at[n, d],
+            device_id=(sides[n], peer), device_id_type=MESH)
+
+    def up_from(n, d):
+        peer = lax.rem(lon + count - d, count)
+        return pltpu.make_async_remote_copy(
+            src_ref=up_ref.at[peer, 1 - n], dst_ref=got[n].at[peer],
+            send_sem=up_send.at[n, d], recv_sem=up_recv.at[n, d],
+            device_id=(sides[1 - n], peer), device_id_type=MESH)
+
+    def down(n, d):
+        peer = lax.rem(lon + d, count)
+        return pltpu.make_async_remote_copy(
+            src_ref=pick.at[n, peer], dst_ref=rows_ref.at[lon, n],
+            send_sem=dn_send.at[n, d], recv_sem=dn_recv.at[n, d],
+            device_id=(lat, peer), device_id_type=MESH)
+
+    def down_from(n, d):
+        peer = lax.rem(lon + count - d, count)
+        return pltpu.make_async_remote_copy(
+            src_ref=pick.at[n, peer], dst_ref=rows_ref.at[peer, n],
+            send_sem=dn_send.at[n, d], recv_sem=dn_recv.at[n, d],
+            device_id=(lat, peer), device_id_type=MESH)
+
+    def each(first, fn):
+        def body(d, carry):
+            fn(d)
+            return carry
+        lax.fori_loop(first, count, body, 0)
+
+    to_e = pltpu.make_async_remote_copy(
+        src_ref=e_ref, dst_ref=from_w, send_sem=we_send.at[0], recv_sem=we_recv.at[0],
+        device_id=(lat, lax.rem(lon + 1, count)), device_id_type=MESH)
+    to_w = pltpu.make_async_remote_copy(
+        src_ref=w_ref, dst_ref=from_e, send_sem=we_send.at[1], recv_sem=we_recv.at[1],
+        device_id=(lat, lax.rem(lon + count - 1, count)), device_id_type=MESH)
+
+    for n in range(2):
+        each(0, lambda d: up(n, d).start())
+    to_e.start()
+    to_w.start()
+    for n in range(2):
+        each(0, lambda d: up_from(n, d).wait_recv())
+
+        def choose(o):
+            value = got[n][tab[2 * n, o]]
+            pick[n, o] = jnp.where(tab[2 * n + 1, o] > 0, value, 0.0)
+
+        each(0, choose)
+        rows_ref[lon, n] = pick[n, lon]
+        each(1, lambda d: down(n, d).start())
+    for n in range(2):
+        each(1, lambda d: down_from(n, d).wait_recv())
+    to_e.wait()
+    to_w.wait()
+    for n in range(2):
+        each(0, lambda d: up(n, d).wait_send())
+        each(1, lambda d: down(n, d).wait_send())
+
+
+def halo(tab, rows, w_out, e_out):
+    anywhere = pl.BlockSpec(memory_space=pl.ANY)
+    here = pl.BlockSpec(memory_space=VM)
+    edge = jax.ShapeDtypeStruct((4, ROWS3, CELLS), jnp.float32)
+    dma = pltpu.SemaphoreType.DMA
+    rows, from_w, from_e = pl.pallas_call(
+        halo_kernel,
+        in_specs=[pl.BlockSpec(memory_space=pltpu.SMEM), here, anywhere, anywhere],
+        out_specs=[here, anywhere, anywhere],
+        out_shape=[jax.ShapeDtypeStruct((16, 2, HALF, 128), jnp.float32), edge, edge],
+        scratch_shapes=[VM((16, HALF, 128), jnp.float32), VM((16, HALF, 128), jnp.float32),
+                        VM((2, 16, HALF, 128), jnp.float32),
+                        dma((2, 16)), dma((2, 16)), dma((2, 16)), dma((2, 16)), dma((2,)), dma((2,))],
+        compiler_params=pltpu.CompilerParams(collective_id=1, has_side_effects=True),
+        cost_estimate=pl.CostEstimate(flops=10**6, bytes_accessed=10**8, transcendentals=0),
+        name="halo",
+    )(tab, rows.reshape(16, 2, HALF, 128), w_out, e_out)
+    return rows.reshape(8, 2, 2, HALF, 128), from_w, from_e
 
 
 def heat_kernel(tab, got, wet, light, out, fine):
@@ -537,6 +629,8 @@
     src = jnp.where(full, block // TILE, 0)
     used = jnp.any((src[None, :] == jnp.arange(16)[:, None]) & full[None, :], axis=1)
     spare = jnp.argmin(used).astype(jnp.int32)
+    pair_used = jnp.any(used.reshape(8, 2), axis=1)
+    pair_spare = jnp.argmin(pair_used).astype(jnp.int32)
     w_slot = jnp.where(full & (west >= 0), west % SLOTS, 0)
     e_slot = jnp.where(full & (east >= 0), east % SLOTS, 0)
     mine = lax.dynamic_slice_in_dim(band, lon * TILE, TILE)
@@ -544,7 +638,22 @@
     t_own = mine // SLOTS % 16
     t_used = jnp.any((t_own[None, :] == jnp.arange(16)[:, None]) & t_wet[None, :], axis=1)
     t_spare = jnp.argmin(t_used).astype(jnp.int32)
-    rows = [src, full, w_slot, e_slot, jnp.where(full, src, spare), t_wet, jnp.where(t_wet, t_own, t_spare), src]
+    rows = [src, full, w_slot, e_slot, jnp.where(full, src, spare), t_wet, jnp.where(t_wet, t_own, t_spare), src // 2, jnp.where(full, src // 2, pair_spare)]
+    return jnp.stack([r.astype(jnp.int32) for r in rows])
+
+
+def meeting(band, south, north, lon):
+    first = lon // 2 * 16
+
+    def cut(row):
+        return lax.dynamic_slice_in_dim(row, first, 16)
+
+    mine = cut(band)
+    hit = ((mine // SLOTS % 16)[None, :] == jnp.arange(16)[:, None]) & (mine >= 0)[None, :]
+    rows = []
+    for other in (cut(south), cut(north)):
+        rows.append(jnp.sum(jnp.where(hit & (other >= 0)[None, :], (other // SLOTS % 16)[None, :], 0), axis=1))
+        rows.append(jnp.any(hit & (other >= 0)[None, :], axis=1))
     return jnp.stack([r.astype(jnp.int32) for r in rows])
 
 
@@ -564,6 +673,8 @@
     wet_n = shift(wet[0], "lat", -1, False)
     wet_w = shift(wet[:, -1], "lon", 1)
     wet_e = shift(wet[:, 0], "lon", -1)
+    band = owner_map[0]
+    meet = meeting(band, shift(band, "lat", 1), shift(band, "lat", -1), lax.axis_index("lon"))
     rows_out, w_out, e_out = pack(tab, tracers)
     open_e = wet * jnp.concatenate([wet[:, 1:], wet_e[:, None]], axis=1)
     open_w = wet * jnp.concatenate([wet_w[:, None], wet[:, :-1]], axis=1)
@@ -580,10 +691,7 @@
     phys = swap(package(tab, y, col, row))
     current = tracers
     for n in range(2):
-        south, north = unpick(tab, swap(rows_out))
-        rows = swap(repick(tab, shift(north, "lat", 1), shift(south, "lat", -1)))
-        came_west = shift(e_out, "lon", 1)
-        came_east = shift(w_out, "lon", -1)
+        rows, came_west, came_east = halo(meet, rows_out, w_out, e_out)
         if n == 0:
             current, rows_out, w_out, e_out = step(False, tab, current, phys, rows, came_west, came_east)
         else:

time: 418 us -> 324 us (0.78)
  the two profiles are of different devices: /device:TPU:4 before, /device:TPU:2 now
where the time goes in v2:
time: 324 us; the launch traced here: 320 us
  Pallas kernels  262 us (81%)
  blocking collectives  19.8 us (6%)
  starting transfers between devices  16.9 us (5%)
  other arithmetic  9.66 us (3%)
  waiting for transfers between devices  6.34 us (2%)
  local copies, waits for them, and re-layouts  3.96 us (1%)
    pallas_call x2, Pallas kernels, halo(): pl.pallas_call(halo_kernel, in_specs=[pl.BlockSpec(memory_space=pltpu.SME...  157 us
    pallas_call x2, Pallas kernels, step(): pl.pallas_call(last_kernel if last else first_kernel, grid_spec=pltpu.Pre...  62.5 us
    all_to_all x1, blocking collectives, swap(): return lax.all_to_all(x, 'lon', split_axis=0, concat_axis=0, tiled=True)  19.8 us
    ppermute x8, starting transfers between devices, shift(): lax.ppermute(x, axis, [(i, (i + by) % n) for i in range(n) if closed or 0...  12.2 us
    pallas_call x1, Pallas kernels, coarse(): pl.pallas_call(coarse_kernel, grid=(SIDE,), in_specs=[pl.BlockSpec((3, 14...  12.2 us
    pallas_call x1, Pallas kernels, heat(): pl.pallas_call(heat_kernel, in_specs=[pl.BlockSpec(memory_space=pltpu.SME...  11.7 us
    pallas_call x1, Pallas kernels, pack(): pl.pallas_call(pack_kernel, grid_spec=pltpu.PrefetchScalarGridSpec(num_sc...  10.6 us
    pallas_call x1, Pallas kernels, package(): pl.pallas_call(package_kernel, grid_spec=pltpu.PrefetchScalarGridSpec(num...  8.03 us
  transfers between devices with their start and end apart: 9, of which 2 were waited for; matrix products, arithmetic and copies ran while one was open for 4% of the time, Pallas kernels for 30%

profile of v2, /device:TPU:2, one launch (start us, length us, event | category | flops | bytes accessed | tf_op | source)
XLA Modules:
  0.0 320.3 jit_solution(4957514478240853311)
XLA Ops:
  1.3 1.9 collective-permute-start.3
  3.3 2.4 collective-permute-start.2
  5.8 6.6 %collective-permute-start.1 = (f32[16]{0:T(128)S(1)}, f32[16]{0:T(128)S(1)}, u32[]{:S(2)}, u32[]{:S(2)}) collective-permute-start(f32[16]{0:T(128)S(1)} %get-tuple-element.42), channel_id=1, source_target_pairs={{0,15},{1,0},{2,1},{3,2},{4,3},{5,4},{6,5},{7,6},{8,7},{9,8},{10,9... | collective-permute-start | bytes 200 | tf_op jit(solution)/shard_map/ppermute | solution.py:662
  12.4 0.8 broadcast_compare_fusion
  13.4 0.9 select_reduce_fusion.2
  14.5 0.7 iota_reduce_fusion.2
  15.3 0.7 fusion.26
  18.9 1.3 convolution_bitcast_fusion
  21.1 0.8 maximum_multiply_fusion.3
  22.6 12.2 %coarse.1 = (f32[16,200,128]{2,1,0:T(8,128)}, f32[48,128]{1,0:T(8,128)}) custom-call(bf16[48,144,384]{2,1,0:T(8,128)(2,1)} %bitcast.75, bf16[16,48,128]{2,1,0:T(8,128)(2,1)} %bitcast.81, f32[16,8,128]{2,1,0:T(8,128)} %stack.52.flags), custom_call_target="tpu_custom_call" | custom-call | flops 1000000000 | bytes 8000000 | tf_op jit(solution)/shard_map/coarse/pallas_call | solution.py:408
  34.8 0.7 slice_bitcast_fusion
  35.6 0.8 collective-permute-start.5
  36.4 1.2 stack.22.tab
  37.6 1.2 collective-permute-done.5.row_ref
  38.8 5.1 %collective-permute-done.4.col_ref = f32[48,128]{1,0:T(8,128)S(1)} collective-permute-done((f32[48,128]{1,0:T(8,128)}, f32[48,128]{1,0:T(8,128)S(1)}, u32[]{:S(2)}, u32[]{:S(2)}) %collective-permute-start.4) | collective-permute-done | bytes 24608 | tf_op jit(solution)/shard_map/ppermute | solution.py:662
  44.5 8.0 %package.1 = f32[16,224,256]{2,1,0:T(8,128)} custom-call(s32[9,8]{1,0:T(8,128)} %stack.22.tab, f32[16,200,128]{2,1,0:T(8,128)} %get-tuple-element.25.y_ref, f32[48,128]{1,0:T(8,128)} %copy-done.2, f32[48,128]{1,0:T(8,128)} %copy-done.1), custom_call_target="tpu_custom_call" | custom-call | flops 10000000 | bytes 4000000 | tf_op jit(solution)/shard_map/package/pallas_call | solution.py:452
  52.6 4.7 %all-to-all-start = ((f32[16,224,256]{2,1,0:T(8,128)}), f32[16,224,256]{2,1,0:T(8,128)}, u32[]{:S(2)}, u32[]{:S(2)}) async-start(f32[16,224,256]{2,1,0:T(8,128)} %package.1), calls=%async_computation | async-start | bytes 7340032 | tf_op jit(solution)/shard_map/all_to_all | solution.py:666
  57.9 10.6 %pack.1 = (f32[8,2,2,72,128]{4,3,2,1,0:T(8,128)}, f32[4,144,256]{2,1,0:T(8,128)}, f32[4,144,256]{2,1,0:T(8,128)}) custom-call(s32[9,8]{1,0:T(8,128)} %stack.22.tab, f32[8,1152,256]{2,1,0:T(8,128)} %c_ref.3), custom_call_target="tpu_custom_call" | custom-call | flops 10000000 | bytes 12000000 | tf_op jit(solution)/shard_map/pack/pallas_call | solution.py:91
  69.7 86.9 %halo.2 = (f32[16,2,72,128]{3,2,1,0:T(8,128)}, f32[4,144,256]{2,1,0:T(8,128)}, f32[4,144,256]{2,1,0:T(8,128)}) custom-call(s32[4,16]{1,0:T(4,128)} %pad_add_fusion.tab, f32[16,2,72,128]{3,2,1,0:T(8,128)} %bitcast.78, f32[4,144,256]{2,1,0:T(8,128)} %get-tuple-element.28.w_ref, f32[4,144,256]{2,1,0:T(8,128)} %get-tuple-element.29.e_ref), custom_call_target="tpu_custom_call" | custom-call | flops 1000000 | bytes 100000000 | tf_op jit(solution)/shard_map/halo/pallas_call | solution.py:564
  156.6 33.1 %first_step.1 = (f32[8,1152,256]{2,1,0:T(8,128)}, f32[8,2,2,72,128]{4,3,2,1,0:T(8,128)}, f32[4,144,256]{2,1,0:T(8,128)}, f32[4,144,256]{2,1,0:T(8,128)}) custom-call(s32[9,8]{1,0:T(8,128)} %stack.22.tab, f32[8,1152,256]{2,1,0:T(8,128)} %c_ref.3, f32[16,224,256]{2,1,0:T(8,128)} %all-to-all-done.phys, f32[8,2,2,72,128]{4,3,2,1,0:T(8,128)} %bitcast.76, ...), custom_call_target="tpu_custom_call" | custom-call | flops 100000000 | bytes 25000000 | tf_op jit(solution)/shard_map/first_step/pallas_call | solution.py:352
  189.7 69.7 %halo.3 = (f32[16,2,72,128]{3,2,1,0:T(8,128)}, f32[4,144,256]{2,1,0:T(8,128)}, f32[4,144,256]{2,1,0:T(8,128)}) custom-call(s32[4,16]{1,0:T(4,128)} %pad_add_fusion.tab, f32[16,2,72,128]{3,2,1,0:T(8,128)} %bitcast.79, f32[4,144,256]{2,1,0:T(8,128)} %get-tuple-element.35.w_ref, f32[4,144,256]{2,1,0:T(8,128)} %get-tuple-element.36.e_ref), custom_call_target="tpu_custom_call" | custom-call | flops 1000000 | bytes 100000000 | tf_op jit(solution)/shard_map/halo/pallas_call | solution.py:564
  259.4 29.4 %last_step.1 = (f32[8,1152,256]{2,1,0:T(8,128)}, f32[16,48,256]{2,1,0:T(8,128)}) custom-call(s32[9,8]{1,0:T(8,128)} %stack.22.tab, f32[8,1152,256]{2,1,0:T(8,128)} %get-tuple-element.33.c_ref, f32[16,224,256]{2,1,0:T(8,128)} %all-to-all-done.phys, f32[8,2,2,72,128]{4,3,2,1,0:T(8,128)} %bitcast.77, f32[4,144,256]{2,1,0:T(8,128)} %get-tuple-element.38.west, ...), custom_call_target="tpu_custom_call" | custom-call | flops 100000000 | bytes 25000000 | tf_op jit(solution)/shard_map/last_step/pallas_call | solution.py:352
  288.8 19.8 %all_to_all.10.got = f32[16,48,256]{2,1,0:T(8,128)} all-to-all(f32[16,48,256]{2,1,0:T(8,128)} %get-tuple-element.41), channel_id=1, replica_groups=mesh['lat'=8,'lon'=16] {'lon'}, dimensions={0} | all-to-all | bytes 1572864 | tf_op jit(solution)/shard_map/all_to_all | solution.py:666
  308.6 11.7 %heat.1 = bf16[48,48,384]{2,1,0:T(8,128)(2,1)} custom-call(s32[9,8]{1,0:T(8,128)} %stack.22.tab, f32[16,48,256]{2,1,0:T(8,128)} %all_to_all.10.got, f32[16,128]{1,0:T(8,128)} %copy-done, f32[48,384]{1,0:T(8,128)} %light.1), custom_call_target="tpu_custom_call" | custom-call | flops 1000000000 | bytes 3000000 | tf_op jit(solution)/shard_map/heat/pallas_call | solution.py:608
  (57 shorter events, 8.3 us)
Async XLA Ops:
  1.3 33.5 %copy-start = (f32[16,128]{1,0:T(8,128)}, f32[16,128]{1,0:T(8,128)S(1)}, u32[]{:S(2)}) copy-start(f32[16,128]{1,0:T(8,128)S(1)} %convert_element_type.46.wet) | copy-start | bytes 24580
  1.3 19.8 %collective-permute-start.3 = (f32[128]{0:T(128)S(1)}, f32[128]{0:T(128)S(1)}, u32[]{:S(2)}, u32[]{:S(2)}) collective-permute-start(f32[128]{0:T(128)S(1)} %get-tuple-element.62), channel_id=1, source_target_pairs={{16,0},{32,16},{48,32},{64,48},{80,64},{96,80},{112,96},{17,1},{33... | collective-permute-start | bytes 1544 | tf_op jit(solution)/shard_map/ppermute | solution.py:662
  3.3 17.8 %collective-permute-start.2 = (f32[128]{0:T(128)S(1)}, f32[128]{0:T(128)S(1)}, u32[]{:S(2)}, u32[]{:S(2)}) collective-permute-start(f32[128]{0:T(128)S(1)} %get-tuple-element.63), channel_id=1, source_target_pairs={{0,16},{16,32},{32,48},{48,64},{64,80},{80,96},{96,112},{1,17},{17... | collective-permute-start | bytes 1544 | tf_op jit(solution)/shard_map/ppermute | solution.py:662
  5.8 15.1 %collective-permute-start.1 = (f32[16]{0:T(128)S(1)}, f32[16]{0:T(128)S(1)}, u32[]{:S(2)}, u32[]{:S(2)}) collective-permute-start(f32[16]{0:T(128)S(1)} %get-tuple-element.42), channel_id=1, source_target_pairs={{0,15},{1,0},{2,1},{3,2},{4,3},{5,4},{6,5},{7,6},{8,7},{9,8},{10,9... | collective-permute-start | bytes 200 | tf_op jit(solution)/shard_map/ppermute | solution.py:662
  12.4 8.6 %collective-permute-start = (f32[16]{0:T(128)S(1)}, f32[16]{0:T(128)S(1)}, u32[]{:S(2)}, u32[]{:S(2)}) collective-permute-start(f32[16]{0:T(128)S(1)} %get-tuple-element.43), channel_id=1, source_target_pairs={{0,1},{1,2},{2,3},{3,4},{4,5},{5,6},{6,7},{7,8},{8,9},{9,10},{10,1... | collective-permute-start | bytes 200 | tf_op jit(solution)/shard_map/ppermute | solution.py:662
  35.6 3.3 %collective-permute-start.5 = (f32[48,128]{1,0:T(8,128)S(1)}, f32[48,128]{1,0:T(8,128)S(1)}, u32[]{:S(2)}, u32[]{:S(2)}) collective-permute-start(f32[48,128]{1,0:T(8,128)S(1)} %slice_bitcast_fusion), channel_id=1, source_target_pairs={{0,16},{16,32},{32,48},{48,64},{64,80},{80,96},{96,112},{112,0},{1... | collective-permute-start | bytes 73736 | tf_op jit(solution)/shard_map/ppermute | solution.py:662
  36.4 7.5 %collective-permute-start.4 = (f32[48,128]{1,0:T(8,128)}, f32[48,128]{1,0:T(8,128)S(1)}, u32[]{:S(2)}, u32[]{:S(2)}) collective-permute-start(f32[48,128]{1,0:T(8,128)} %get-tuple-element.26), channel_id=1, source_target_pairs={{0,1},{1,2},{2,3},{3,4},{4,5},{5,6},{6,7},{7,8},{8,9},{9,10},{10,1... | collective-permute-start | bytes 73736 | tf_op jit(solution)/shard_map/ppermute | solution.py:662
  38.8 5.1 %copy-start.1 = (f32[48,128]{1,0:T(8,128)}, f32[48,128]{1,0:T(8,128)S(1)}, u32[]{:S(2)}) copy-start(f32[48,128]{1,0:T(8,128)S(1)} %collective-permute-done.5.row_ref) | copy-start | bytes 73732
  43.9 0.6 copy-start.2
  52.6 4.7 %copy-start.3 = (s32[1,128]{1,0:T(1,128)S(1)}, s32[1,128]{1,0:T(1,128)}, u32[]{:S(2)}) copy-start(s32[1,128]{1,0:T(1,128)} %param.11) | copy-start | bytes 1540
  52.6 104.0 %all-to-all-start = ((f32[16,224,256]{2,1,0:T(8,128)}), f32[16,224,256]{2,1,0:T(8,128)}, u32[]{:S(2)}, u32[]{:S(2)}) async-start(f32[16,224,256]{2,1,0:T(8,128)} %package.1), calls=%async_computation | async-start | bytes 7340032 | tf_op jit(solution)/shard_map/all_to_all | solution.py:666
  57.2 11.3 %collective-permute-start.7 = (s32[128]{0:T(128)S(1)}, s32[128]{0:T(128)S(1)}, u32[]{:S(2)}, u32[]{:S(2)}) collective-permute-start(s32[128]{0:T(128)S(1)} %bitcast.88), channel_id=1, source_target_pairs={{0,112},{16,0},{32,16},{48,32},{64,48},{80,64},{96,80},{112,96},{1... | collective-permute-start | bytes 1544 | tf_op jit(solution)/shard_map/ppermute | solution.py:662
  57.5 11.2 %collective-permute-start.6 = (s32[128]{0:T(128)S(1)}, s32[128]{0:T(128)S(1)}, u32[]{:S(2)}, u32[]{:S(2)}) collective-permute-start(s32[128]{0:T(128)S(1)} %bitcast.89), channel_id=1, source_target_pairs={{0,16},{16,32},{32,48},{48,64},{64,80},{80,96},{96,112},{112,0},{1... | collective-permute-start | bytes 1544 | tf_op jit(solution)/shard_map/ppermute | solution.py:662

commit v3 on v2

--- a/solution.py
+++ b/solution.py
@@ -356,7 +356,7 @@
             grid=(SLOTS,),
             in_specs=[
                 pl.BlockSpec((1, NTR * LEV, CELLS), lambda j, tab: (j, 0, 0)),
-                pl.BlockSpec((1, PHYS, CELLS), lambda j, tab: (tab[0, j], 0, 0)),
+                pl.BlockSpec((1, PHYS, CELLS), lambda j, tab: (tab[10, j], 0, 0)),
                 pl.BlockSpec((1, 2, 2, HALF, 128), lambda j, tab: (tab[7, j], 0, 0, 0, 0)),
                 pl.BlockSpec((1, ROWS3, CELLS), lambda j, tab: (tab[2, j] // 2, 0, 0)),
                 pl.BlockSpec((1, ROWS3, CELLS), lambda j, tab: (tab[3, j] // 2, 0, 0)),
@@ -377,50 +377,57 @@
     return (i // 3 == j if lhs_wide else i == j // 3).astype(dtype)
 
 
-def coarse_kernel(phys, mix, flags, y_ref, col_ref):
-    r = pl.program_id(0)
-    i = lax.broadcasted_iota(jnp.int32, (384, 128), 0)
-    j = lax.broadcasted_iota(jnp.int32, (384, 128), 1)
-    every = (i // 3 == j).astype(jnp.bfloat16)
-    third = (i == 3 * j + 2).astype(jnp.bfloat16)
+def coarse_kernel(phys, mix, flags, y_ref, col_ref, every_ref, third_ref):
+    step = pl.program_id(0)
+
+    @pl.when(step == 0)
+    def _():
+        i = lax.broadcasted_iota(jnp.int32, (384, 128), 0)
+        j = lax.broadcasted_iota(jnp.int32, (384, 128), 1)
+        every_ref[...] = (i // 3 == j).astype(jnp.bfloat16)
+        third_ref[...] = (i == 3 * j + 2).astype(jnp.bfloat16)
+        col_ref[...] = jnp.zeros_like(col_ref)
 
     def dot(a, b):
         return jnp.dot(a, b, preferred_element_type=jnp.float32)
 
-    east = (dot(phys[0, 0:48, :], third) + dot(phys[1, 0:48, :], third) + dot(phys[2, 0:48, :], third)) / 3.0
-    north = dot(phys[2, 48:96, :], every) / 3.0
-    temp = (dot(phys[0, 96:144, :], every) + dot(phys[1, 96:144, :], every) + dot(phys[2, 96:144, :], every)) / 9.0
-    east = east * flags[0, 1:2, :]
-    y_ref[0, 0:48, :] = east
-    y_ref[0, 48:96, :] = north * flags[0, 3:4, :]
-    y_ref[0, 96:144, :] = temp
-    y_ref[0, 144:192, :] = mix[0].astype(jnp.float32)
-    y_ref[0, 192:200, :] = flags[0]
-
-    @pl.when(r == 0)
-    def _():
-        col_ref[...] = jnp.zeros_like(col_ref)
-
-    col_ref[...] = jnp.where(lanes() == r, roll(east, r + 1), col_ref[...])
+    u = jnp.concatenate([phys[f, 0:48, :] for f in range(6)], axis=0)
+    vt = jnp.concatenate([phys[2, 48:96, :], phys[5, 48:96, :]] + [phys[f, 96:144, :] for f in range(6)], axis=0)
+    east = dot(u, third_ref[...])
+    rest = dot(vt, every_ref[...])
+
+    def part(x, n):
+        return x[48 * n:48 * n + 48]
+
+    for c in range(2):
+        e = (part(east, 3 * c) + part(east, 3 * c + 1) + part(east, 3 * c + 2)) / 3.0 * flags[c, 1:2, :]
+        y_ref[c, 0:48, :] = e
+        y_ref[c, 48:96, :] = part(rest, c) / 3.0 * flags[c, 3:4, :]
+        y_ref[c, 96:144, :] = (part(rest, 3 * c + 2) + part(rest, 3 * c + 3) + part(rest, 3 * c + 4)) / 9.0
+        y_ref[c, 144:192, :] = mix[c].astype(jnp.float32)
+        y_ref[c, 192:200, :] = flags[c]
+        r = 2 * step + c
+        col_ref[...] = jnp.where(lanes() == r, roll(e, r + 1), col_ref[...])
 
 
 def coarse(phys_t, mix_t, flags):
     return pl.pallas_call(
         coarse_kernel,
-        grid=(SIDE,),
+        grid=(SIDE // 2,),
         in_specs=[
-            pl.BlockSpec((3, 144, 384), lambda r: (r, 0, 0)),
-            pl.BlockSpec((1, LEV, 128), lambda r: (r, 0, 0)),
-            pl.BlockSpec((1, 8, 128), lambda r: (r, 0, 0)),
+            pl.BlockSpec((6, 144, 384), lambda r: (r, 0, 0)),
+            pl.BlockSpec((2, LEV, 128), lambda r: (r, 0, 0)),
+            pl.BlockSpec((2, 8, 128), lambda r: (r, 0, 0)),
         ],
         out_specs=[
-            pl.BlockSpec((1, 200, 128), lambda r: (r, 0, 0)),
+            pl.BlockSpec((2, 200, 128), lambda r: (r, 0, 0)),
             pl.BlockSpec((LEV, 128), lambda r: (0, 0)),
         ],
         out_shape=[
             jax.ShapeDtypeStruct((SIDE, 200, 128), jnp.float32),
             jax.ShapeDtypeStruct((LEV, 128), jnp.float32),
         ],
+        scratch_shapes=[VM((384, 128), jnp.bfloat16), VM((384, 128), jnp.bfloat16)],
         cost_estimate=pl.CostEstimate(flops=10**9, bytes_accessed=8 * 10**6, transcendentals=0),
         name="coarse",
     )(phys_t, mix_t, flags)
@@ -459,9 +466,9 @@
                 pl.BlockSpec((LEV, 128), lambda k, tab: (0, 0)),
                 pl.BlockSpec((LEV, 128), lambda k, tab: (0, 0)),
             ],
-            out_specs=pl.BlockSpec((1, PHYS, CELLS), lambda k, tab: (tab[6, k], 0, 0)),
+            out_specs=pl.BlockSpec((1, PHYS, CELLS), lambda k, tab: (tab[9, k], 0, 0)),
         ),
-        out_shape=jax.ShapeDtypeStruct((16, PHYS, CELLS), jnp.float32),
+        out_shape=jax.ShapeDtypeStruct((8, PHYS, CELLS), jnp.float32),
         cost_estimate=pl.CostEstimate(flops=10**7, bytes_accessed=4 * 10**6, transcendentals=0),
         name="package",
     )(tab, y, col, row)
@@ -470,110 +477,152 @@
 MESH = pl.DeviceIdType.MESH
 
 
-def halo_kernel(tab, up_ref, w_ref, e_ref, rows_ref, from_w, from_e, got_s, got_n, pick,
-                up_send, up_recv, dn_send, dn_recv, we_send, we_recv):
+def remote(src, dst, send, recv, where):
+    return pltpu.make_async_remote_copy(src_ref=src, dst_ref=dst, send_sem=send, recv_sem=recv,
+                                        device_id=where, device_id_type=MESH)
+
+
+def each(first, last, fn):
+    def body(d, carry):
+        fn(d)
+        return carry
+    lax.fori_loop(first, last, body, 0)
+
+
+def halo_kernel(first, *refs):
+    if first:
+        (tab, up_ref, phys, rows_ref, phys_out, got_s, got_n, pick, mid, turn,
+         up_send, up_recv, dn_send, dn_recv, z_send, z_recv, y_send, y_recv, own) = refs
+    else:
+        (tab, up_ref, w_ref, e_ref, rows_ref, from_w, from_e, got_s, got_n, pick,
+         up_send, up_recv, dn_send, dn_recv, we_send, we_recv) = refs
     lat, lon = lax.axis_index("lat"), lax.axis_index("lon")
     bands, count = lax.axis_size("lat"), lax.axis_size("lon")
     sides = (lax.rem(lat + 1, bands), lax.rem(lat + bands - 1, bands))
+    row, place = lon // 4, lax.rem(lon, 4)
     got = (got_s, got_n)
     barrier = pltpu.get_barrier_semaphore()
 
-    def greet(d, carry):
+    def greet(d):
         peer = lax.rem(lon + d, count)
         for side in sides:
             pl.semaphore_signal(barrier, inc=1, device_id=(side, peer), device_id_type=MESH)
-        return carry
-
-    def greet_band(d, carry):
-        pl.semaphore_signal(barrier, inc=1, device_id=(lat, lax.rem(lon + d, count)), device_id_type=MESH)
-        return carry
-
-    lax.fori_loop(0, count, greet, 0)
-    lax.fori_loop(1, count, greet_band, 0)
+
+    each(0, count, greet)
+    each(1, count, lambda d: pl.semaphore_signal(
+        barrier, inc=1, device_id=(lat, lax.rem(lon + d, count)), device_id_type=MESH))
     pl.semaphore_wait(barrier, 3 * count - 1)
 
     def up(n, d):
         peer = lax.rem(lon + d, count)
-        return pltpu.make_async_remote_copy(
-            src_ref=up_ref.at[peer, 1 - n], dst_ref=got[n].at[lon],
-            send_sem=up_send.at[n, d], recv_sem=up_recv.at[n, d],
-            device_id=(sides[n], peer), device_id_type=MESH)
+        return remote(up_ref.at[peer, 1 - n], got[n].at[lon], up_send.at[n, d], up_recv.at[n, d], (sides[n], peer))
 
     def up_from(n, d):
         peer = lax.rem(lon + count - d, count)
-        return pltpu.make_async_remote_copy(
-            src_ref=up_ref.at[peer, 1 - n], dst_ref=got[n].at[peer],
-            send_sem=up_send.at[n, d], recv_sem=up_recv.at[n, d],
-            device_id=(sides[1 - n], peer), device_id_type=MESH)
+        return remote(up_ref.at[peer, 1 - n], got[n].at[peer], up_send.at[n, d], up_recv.at[n, d], (sides[1 - n], peer))
 
     def down(n, d):
         peer = lax.rem(lon + d, count)
-        return pltpu.make_async_remote_copy(
-            src_ref=pick.at[n, peer], dst_ref=rows_ref.at[lon, n],
-            send_sem=dn_send.at[n, d], recv_sem=dn_recv.at[n, d],
-            device_id=(lat, peer), device_id_type=MESH)
+        return remote(pick.at[n, peer], rows_ref.at[lon, n], dn_send.at[n, d], dn_recv.at[n, d], (lat, peer))
 
     def down_from(n, d):
         peer = lax.rem(lon + count - d, count)
-        return pltpu.make_async_remote_copy(
-            src_ref=pick.at[n, peer], dst_ref=rows_ref.at[peer, n],
-            send_sem=dn_send.at[n, d], recv_sem=dn_recv.at[n, d],
-            device_id=(lat, peer), device_id_type=MESH)
-
-    def each(first, fn):
-        def body(d, carry):
-            fn(d)
-            return carry
-        lax.fori_loop(first, count, body, 0)
-
-    to_e = pltpu.make_async_remote_copy(
-        src_ref=e_ref, dst_ref=from_w, send_sem=we_send.at[0], recv_sem=we_recv.at[0],
-        device_id=(lat, lax.rem(lon + 1, count)), device_id_type=MESH)
-    to_w = pltpu.make_async_remote_copy(
-        src_ref=w_ref, dst_ref=from_e, send_sem=we_send.at[1], recv_sem=we_recv.at[1],
-        device_id=(lat, lax.rem(lon + count - 1, count)), device_id_type=MESH)
-
-    for n in range(2):
-        each(0, lambda d: up(n, d).start())
-    to_e.start()
-    to_w.start()
-    for n in range(2):
-        each(0, lambda d: up_from(n, d).wait_recv())
+        return remote(pick.at[n, peer], rows_ref.at[peer, n], dn_send.at[n, d], dn_recv.at[n, d], (lat, peer))
+
+    def by_z(d):
+        z = lax.rem(place + d, 4)
+        return remote(phys.at[z], mid.at[place], z_send.at[d], z_recv.at[d], (lat, 4 * row + z))
+
+    def from_z(d):
+        z = lax.rem(place + 4 - d, 4)
+        return remote(phys.at[z], mid.at[z], z_send.at[d], z_recv.at[d], (lat, 4 * row + z))
+
+    def by_y(d):
+        y = lax.rem(row + d, 4)
+        return remote(turn.at[y], phys_out.at[row], y_send.at[d], y_recv.at[d], (lat, 4 * y + place))
+
+    def from_y(d):
+        y = lax.rem(row + 4 - d, 4)
+        return remote(turn.at[y], phys_out.at[y], y_send.at[d], y_recv.at[d], (lat, 4 * y + place))
+
+    def descend(n):
+        each(0, count, lambda d: up_from(n, d).wait_recv())
 
         def choose(o):
             value = got[n][tab[2 * n, o]]
             pick[n, o] = jnp.where(tab[2 * n + 1, o] > 0, value, 0.0)
 
-        each(0, choose)
+        each(0, count, choose)
         rows_ref[lon, n] = pick[n, lon]
-        each(1, lambda d: down(n, d).start())
+        each(1, count, lambda d: down(n, d).start())
+
+    if first:
+        each(1, 4, lambda d: by_z(d).start())
+        keep = pltpu.make_async_copy(phys.at[place], mid.at[place], own.at[0])
+        keep.start()
     for n in range(2):
-        each(1, lambda d: down_from(n, d).wait_recv())
-    to_e.wait()
-    to_w.wait()
+        each(0, count, lambda d: up(n, d).start())
+    if first:
+        each(1, 4, lambda d: from_z(d).wait_recv())
+        keep.wait()
+
+        def sort(q):
+            turn[q // 2, lax.rem(q, 2)] = mid[tab[4, q] // 2, lax.rem(tab[4, q], 2)]
+
+        each(0, 8, sort)
+        each(1, 4, lambda d: by_y(d).start())
+        phys_out[row] = turn[row]
+    else:
+        to_e = remote(e_ref, from_w, we_send.at[0], we_recv.at[0], (lat, lax.rem(lon + 1, count)))
+        to_w = remote(w_ref, from_e, we_send.at[1], we_recv.at[1], (lat, lax.rem(lon + count - 1, count)))
+        to_e.start()
+        to_w.start()
+    descend(0)
+    descend(1)
     for n in range(2):
-        each(0, lambda d: up(n, d).wait_send())
-        each(1, lambda d: down(n, d).wait_send())
-
-
-def halo(tab, rows, w_out, e_out):
+        each(1, count, lambda d: down_from(n, d).wait_recv())
+    for n in range(2):
+        each(0, count, lambda d: up(n, d).wait_send())
+        each(1, count, lambda d: down(n, d).wait_send())
+    if first:
+        each(1, 4, lambda d: from_y(d).wait_recv())
+        each(1, 4, lambda d: by_z(d).wait_send())
+        each(1, 4, lambda d: by_y(d).wait_send())
+    else:
+        to_e.wait()
+        to_w.wait()
+
+
+def halo(first, tab, rows, *rest):
     anywhere = pl.BlockSpec(memory_space=pl.ANY)
     here = pl.BlockSpec(memory_space=VM)
     edge = jax.ShapeDtypeStruct((4, ROWS3, CELLS), jnp.float32)
     dma = pltpu.SemaphoreType.DMA
-    rows, from_w, from_e = pl.pallas_call(
-        halo_kernel,
-        in_specs=[pl.BlockSpec(memory_space=pltpu.SMEM), here, anywhere, anywhere],
-        out_specs=[here, anywhere, anywhere],
-        out_shape=[jax.ShapeDtypeStruct((16, 2, HALF, 128), jnp.float32), edge, edge],
-        scratch_shapes=[VM((16, HALF, 128), jnp.float32), VM((16, HALF, 128), jnp.float32),
-                        VM((2, 16, HALF, 128), jnp.float32),
-                        dma((2, 16)), dma((2, 16)), dma((2, 16)), dma((2, 16)), dma((2,)), dma((2,))],
-        compiler_params=pltpu.CompilerParams(collective_id=1, has_side_effects=True),
+    sent = pltpu.VMEM((4, 2, PHYS, CELLS), jnp.float32)
+    out = [jax.ShapeDtypeStruct((16, 2, HALF, 128), jnp.float32)]
+    scratch = [VM((16, HALF, 128), jnp.float32), VM((16, HALF, 128), jnp.float32),
+               VM((2, 16, HALF, 128), jnp.float32)]
+    sems = [dma((2, 16)), dma((2, 16)), dma((2, 16)), dma((2, 16))]
+    if first:
+        in_specs, out_specs = [here], [here, here]
+        out.append(jax.ShapeDtypeStruct((4, 2, PHYS, CELLS), jnp.float32))
+        scratch += [sent, sent] + sems + [dma((4,)), dma((4,)), dma((4,)), dma((4,)), dma((1,))]
+        rest = [rest[0].reshape(4, 2, PHYS, CELLS)]
+    else:
+        in_specs, out_specs = [anywhere] * 2, [here] + [anywhere] * 2
+        out += [edge, edge]
+        scratch += sems + [dma((2,)), dma((2,))]
+    rows, *more = pl.pallas_call(
+        functools.partial(halo_kernel, first),
+        in_specs=[pl.BlockSpec(memory_space=pltpu.SMEM), here] + in_specs,
+        out_specs=out_specs,
+        out_shape=out,
+        scratch_shapes=scratch,
+        compiler_params=pltpu.CompilerParams(collective_id=1 if first else 2, has_side_effects=True),
         cost_estimate=pl.CostEstimate(flops=10**6, bytes_accessed=10**8, transcendentals=0),
-        name="halo",
-    )(tab, rows.reshape(16, 2, HALF, 128), w_out, e_out)
-    return rows.reshape(8, 2, 2, HALF, 128), from_w, from_e
+        name="halo_phys" if first else "halo",
+    )(tab, rows.reshape(16, 2, HALF, 128), *rest)
+    return [rows.reshape(8, 2, 2, HALF, 128)] + more
 
 
 def heat_kernel(tab, got, wet, light, out, fine):
@@ -590,18 +639,19 @@
     spread = spread_matrix((128, 384), False)
     stacked = jnp.concatenate([spread] * 3, axis=0)
 
-    def level(l, carry):
-        x = fine[pl.ds(pl.multiple_of(l * LEV, LEV), LEV), :]
+    def levels(i, carry):
+        x = fine[pl.ds(pl.multiple_of(i * 8 * LEV, 8 * LEV), 8 * LEV), :]
         high = x.astype(jnp.bfloat16)
         rest = x - high.astype(jnp.float32)
         mid = rest.astype(jnp.bfloat16)
         low = (rest - mid.astype(jnp.float32)).astype(jnp.bfloat16)
         wide = jnp.dot(jnp.concatenate([high, mid, low], axis=1), stacked,
                        preferred_element_type=jnp.float32)
-        out[l] = (light[...] * wide).astype(jnp.bfloat16)
+        for l in range(8):
+            out[8 * i + l] = (light[...] * wide[l * LEV:l * LEV + LEV]).astype(jnp.bfloat16)
         return carry
 
-    lax.fori_loop(0, LEV, level, 0)
+    lax.fori_loop(0, LEV // 8, levels, 0)
 
 
 def heat(tab, got, wet, light):
@@ -638,11 +688,26 @@
     t_own = mine // SLOTS % 16
     t_used = jnp.any((t_own[None, :] == jnp.arange(16)[:, None]) & t_wet[None, :], axis=1)
     t_spare = jnp.argmin(t_used).astype(jnp.int32)
-    rows = [src, full, w_slot, e_slot, jnp.where(full, src, spare), t_wet, jnp.where(t_wet, t_own, t_spare), src // 2, jnp.where(full, src // 2, pair_spare)]
-    return jnp.stack([r.astype(jnp.int32) for r in rows])
-
-
-def meeting(band, south, north, lon):
+    ids = jnp.arange(128)
+    before = (ids[None, :] < ids[:, None]) & wet[None, :]
+    near = before & (tile[None, :] == tile[:, None]) & ((owner % 4)[None, :] == (owner % 4)[:, None])
+    near = jnp.sum(near.astype(jnp.int32), axis=1)
+    far = before & ((ids // 32)[None, :] == (ids // 32)[:, None]) & (owner[None, :] == owner[:, None])
+    far = jnp.sum(far.astype(jnp.int32), axis=1)
+    my_near = lax.dynamic_slice_in_dim(near, lon * TILE, TILE)
+    z_at = (t_own % 4) * 2 + my_near
+    z_used = jnp.any((z_at[None, :] == jnp.arange(8)[:, None]) & t_wet[None, :], axis=1)
+    z_at = jnp.where(t_wet, z_at, jnp.argmin(z_used).astype(jnp.int32))
+    got_at = jnp.sum(jnp.where(hit, (ids // 32 * 2 + far)[None, :], 0), axis=1)
+    turn = wet & (ids // 32 == lon // 4) & (owner % 4 == lon % 4)
+    turn = turn[None, :] & ((owner // 4 * 2 + far)[None, :] == jnp.arange(8)[:, None])
+    turn_from = jnp.sum(jnp.where(turn, (tile % 4 * 2 + near)[None, :], 0), axis=1)
+    rows = [src, full, w_slot, e_slot, jnp.where(full, src, spare), t_wet, jnp.where(t_wet, t_own, t_spare),
+            src // 2, jnp.where(full, src // 2, pair_spare), z_at, got_at]
+    return jnp.stack([r.astype(jnp.int32) for r in rows]), turn_from
+
+
+def meeting(band, south, north, lon, turn_from):
     first = lon // 2 * 16
 
     def cut(row):
@@ -654,6 +719,7 @@
     for other in (cut(south), cut(north)):
         rows.append(jnp.sum(jnp.where(hit & (other >= 0)[None, :], (other // SLOTS % 16)[None, :], 0), axis=1))
         rows.append(jnp.any(hit & (other >= 0)[None, :], axis=1))
+    rows.append(jnp.concatenate([turn_from, turn_from]))
     return jnp.stack([r.astype(jnp.int32) for r in rows])
 
 
@@ -667,15 +733,19 @@
 
 
 def on_device(tracers, phys_fine, mix_coarse, surf_light, land_mask, owner_map):
-    tab = tables(owner_map[0], lax.axis_index("lat"), lax.axis_index("lon"))
     wet = land_mask.astype(jnp.float32)
-    wet_s = shift(wet[-1], "lat", 1, False)
-    wet_n = shift(wet[0], "lat", -1, False)
+    band = owner_map[0]
+    codes = band.astype(jnp.float32)
+    width = wet.shape[1]
+    south_in = shift(jnp.concatenate([wet[-1], codes]), "lat", 1)
+    north_in = shift(jnp.concatenate([wet[0], codes]), "lat", -1)
     wet_w = shift(wet[:, -1], "lon", 1)
     wet_e = shift(wet[:, 0], "lon", -1)
-    band = owner_map[0]
-    meet = meeting(band, shift(band, "lat", 1), shift(band, "lat", -1), lax.axis_index("lon"))
-    rows_out, w_out, e_out = pack(tab, tracers)
+    lat, lon = lax.axis_index("lat"), lax.axis_index("lon")
+    tab, turn_from = tables(band, lat, lon)
+    wet_s = jnp.where(lat > 0, south_in[:width], 0.0)
+    wet_n = jnp.where(lat < lax.axis_size("lat") - 1, north_in[:width], 0.0)
+    meet = meeting(band, south_in[width:].astype(jnp.int32), north_in[width:].astype(jnp.int32), lon, turn_from)
     open_e = wet * jnp.concatenate([wet[:, 1:], wet_e[:, None]], axis=1)
     open_w = wet * jnp.concatenate([wet_w[:, None], wet[:, :-1]], axis=1)
     open_n = wet * jnp.concatenate([wet[1:], wet_n[None]], axis=0)
@@ -686,16 +756,19 @@
     blank = jnp.zeros_like(wet)
     flags = jnp.stack([open_w, open_e, open_s, open_n, light, wet, blank, blank], axis=1)
     y, col = coarse(jnp.swapaxes(phys_fine, 1, 2), jnp.swapaxes(mix_coarse, 1, 2), flags)
-    col = shift(col, "lon", 1)
-    row = shift(y[SIDE - 1, 48:96], "lat", 1)
-    phys = swap(package(tab, y, col, row))
-    current = tracers
-    for n in range(2):
-        rows, came_west, came_east = halo(meet, rows_out, w_out, e_out)
-        if n == 0:
-            current, rows_out, w_out, e_out = step(False, tab, current, phys, rows, came_west, came_east)
-        else:
-            current, light_part = step(True, tab, current, phys, rows, came_west, came_east)
+    tab, y, col = lax.optimization_barrier((tab, y, col))
+    west_col = shift(col, "lon", 1)
+    south_row = shift(y[SIDE - 1, 48:96], "lat", 1)
+    rows_out, w_out, e_out = pack(tab, tracers)
+    came_west = shift(e_out, "lon", 1)
+    came_east = shift(w_out, "lon", -1)
+    y, rows_out = lax.optimization_barrier((y, rows_out))
+    packed = package(tab, y, west_col, south_row)
+    rows, phys = halo(True, meet, rows_out, packed)
+    phys = phys.reshape(8, PHYS, CELLS)
+    current, rows_out, w_out, e_out = step(False, tab, tracers, phys, rows, came_west, came_east)
+    rows, came_west, came_east = halo(False, meet, rows_out, w_out, e_out)
+    current, light_part = step(True, tab, current, phys, rows, came_west, came_east)
     return current, heat(tab, swap(light_part), wet, surf_light)
 
 

time: 324 us -> 293 us (0.904)
  Pallas kernels: 262 us -> 229 us
  waiting for transfers between devices: 6.34 us -> 0.02 us
  other arithmetic: 9.66 us -> 14.2 us
  starting transfers between devices: 16.9 us -> 13.5 us
    pallas_call x3, Pallas kernels: 169 us -> 143 us  [the longest x2 136 us: halo(): pl.pallas_call(functools.partial(halo_kernel, first), in_specs=[pl.BlockS...]
    pallas_call x1, Pallas kernels: 11.7 us -> 5.21 us  [heat(): pl.pallas_call(heat_kernel, in_specs=[pl.BlockSpec(memory_space=pltpu.SME...]
    ppermute x8, waiting for transfers between devices: 6.34 us -> 0.02 us  [shift(): lax.ppermute(x, axis, [(i, (i + by) % n) for i in range(n) if closed or 0...]
    all_to_all x1 -> x0, starting transfers between devices: 4.66 us -> none  [swap(): return lax.all_to_all(x, 'lon', split_axis=0, concat_axis=0, tiled=True)]
  transfers between devices with their start and end apart: 9 -> 8, of which waited for: 2 -> 0; matrix products, arithmetic and copies ran while one was open for 4% -> 6% of each run, Pallas kernels for 30% -> 34%
where the time goes in v3:
time: 293 us; the launch traced here: 288 us
  Pallas kernels  229 us (78%)
  blocking collectives  22.3 us (8%)
  other arithmetic  14.2 us (5%)
  starting transfers between devices  13.5 us (5%)
  local copies, waits for them, and re-layouts  6.12 us (2%)
    pallas_call x2, Pallas kernels, halo(): pl.pallas_call(functools.partial(halo_kernel, first), in_specs=[pl.BlockS...  136 us
    pallas_call x2, Pallas kernels, step(): pl.pallas_call(last_kernel if last else first_kernel, grid_spec=pltpu.Pre...  62.5 us
    all_to_all x1, blocking collectives, swap(): return lax.all_to_all(x, 'lon', split_axis=0, concat_axis=0, tiled=True)  22.3 us
    ppermute x8, starting transfers between devices, shift(): lax.ppermute(x, axis, [(i, (i + by) % n) for i in range(n) if closed or 0...  13.5 us
    pallas_call x1, Pallas kernels, pack(): pl.pallas_call(pack_kernel, grid_spec=pltpu.PrefetchScalarGridSpec(num_sc...  10.6 us
    pallas_call x1, Pallas kernels, package(): pl.pallas_call(package_kernel, grid_spec=pltpu.PrefetchScalarGridSpec(num...  8.03 us
    pallas_call x1, Pallas kernels, coarse(): pl.pallas_call(coarse_kernel, grid=(SIDE // 2,), in_specs=[pl.BlockSpec((...  7.35 us
  transfers between devices with their start and end apart: 8, of which 0 were waited for; matrix products, arithmetic and copies ran while one was open for 6% of the time, Pallas kernels for 34%

profile of v3, /device:TPU:2, one launch (start us, length us, event | category | flops | bytes accessed | tf_op | source)
XLA Modules:
  0.0 287.5 jit_solution(7652237876473222187)
XLA Ops:
  1.5 6.5 %collective-permute-start.1 = (f32[16]{0:T(128)S(1)}, f32[16]{0:T(128)S(1)}, u32[]{:S(2)}, u32[]{:S(2)}) collective-permute-start(f32[16]{0:T(128)S(1)} %get-tuple-element.52), channel_id=1, source_target_pairs={{0,15},{1,0},{2,1},{3,2},{4,3},{5,4},{6,5},{7,6},{8,7},{9,8},{10,9... | collective-permute-start | bytes 200 | tf_op jit(solution)/shard_map/ppermute | solution.py:728
  9.3 0.7 fusion.31
  10.0 0.7 compare_bitcast_fusion
  12.4 0.8 broadcast_compare_fusion
  13.4 0.9 select_reduce_fusion.3
  14.5 0.7 iota_reduce_fusion.3
  15.3 0.8 fusion.30
  20.3 1.3 convolution_bitcast_fusion
  22.5 1.2 stack.56.tab
  24.2 0.8 maximum_multiply_fusion.3
  24.9 0.7 stack.63.flags
  25.7 7.4 %coarse.1 = (f32[16,200,128]{2,1,0:T(8,128)}, f32[48,128]{1,0:T(8,128)}) custom-call(bf16[48,144,384]{2,1,0:T(8,128)(2,1)} %bitcast.114, bf16[16,48,128]{2,1,0:T(8,128)(2,1)} %bitcast.120, f32[16,8,128]{2,1,0:T(8,128)} %stack.63.flags), custom_call_target="tpu_custom_call" | custom-call | flops 1000000000 | bytes 8000000 | tf_op jit(solution)/shard_map/coarse/pallas_call | solution.py:414
  33.0 0.7 slice_bitcast_fusion
  33.7 1.1 collective-permute-start.5
  34.9 10.6 %pack.1 = (f32[8,2,2,72,128]{4,3,2,1,0:T(8,128)}, f32[4,144,256]{2,1,0:T(8,128)}, f32[4,144,256]{2,1,0:T(8,128)}) custom-call(s32[11,8]{1,0:T(8,128)} %stack.56.tab, f32[8,1152,256]{2,1,0:T(8,128)} %c_ref.3), custom_call_target="tpu_custom_call" | custom-call | flops 10000000 | bytes 12000000 | tf_op jit(solution)/shard_map/pack/pallas_call | solution.py:91
  45.5 5.3 %collective-permute-start.7 = (f32[4,144,256]{2,1,0:T(8,128)}, f32[4,144,256]{2,1,0:T(8,128)S(1)}, u32[]{:S(2)}, u32[]{:S(2)}) collective-permute-start(f32[4,144,256]{2,1,0:T(8,128)} %get-tuple-element.42), channel_id=1, source_target_pairs={{0,15},{1,0},{2,1},{3,2},{4,3},{5,4},{6,5},{7,6},{8,7},{9,8},{10,9... | collective-permute-start | bytes 1769480 | tf_op jit(solution)/shard_map/ppermute | solution.py:728
  52.9 8.0 %package.1 = f32[8,224,256]{2,1,0:T(8,128)} custom-call(s32[11,8]{1,0:T(8,128)} %stack.56.tab, f32[16,200,128]{2,1,0:T(8,128)} %get-tuple-element.37.y_ref, f32[48,128]{1,0:T(8,128)} %copy-done.4, f32[48,128]{1,0:T(8,128)} %copy-done.3), custom_call_target="tpu_custom_call" | custom-call | flops 10000000 | bytes 4000000 | tf_op jit(solution)/shard_map/package/pallas_call | solution.py:459
  60.9 78.6 %halo_phys.1 = (f32[16,2,72,128]{3,2,1,0:T(8,128)}, f32[4,2,224,256]{3,2,1,0:T(8,128)}) custom-call(s32[5,16]{1,0:T(8,128)} %stack.67.refs_0_, f32[16,2,72,128]{3,2,1,0:T(8,128)} %bitcast.117, f32[4,2,224,256]{3,2,1,0:T(8,128)} %bitcast.111), custom_call_target="tpu_custom_call" | custom-call | flops 1000000 | bytes 100000000 | tf_op jit(solution)/shard_map/halo_phys/pallas_call | solution.py:615
  139.6 0.8 copy-done
  140.6 33.1 %first_step.1 = (f32[8,1152,256]{2,1,0:T(8,128)}, f32[8,2,2,72,128]{4,3,2,1,0:T(8,128)}, f32[4,144,256]{2,1,0:T(8,128)}, f32[4,144,256]{2,1,0:T(8,128)}) custom-call(s32[11,8]{1,0:T(8,128)} %stack.56.tab, f32[8,1152,256]{2,1,0:T(8,128)} %c_ref.3, f32[8,224,256]{2,1,0:T(8,128)} %bitcast.112, f32[8,2,2,72,128]{4,3,2,1,0:T(8,128)} %bitcast.115, ...), custom_call_target="tpu_custom_call" | custom-call | flops 100000000 | bytes 25000000 | tf_op jit(solution)/shard_map/first_step/pallas_call | solution.py:352
  173.6 57.0 %halo.1 = (f32[16,2,72,128]{3,2,1,0:T(8,128)}, f32[4,144,256]{2,1,0:T(8,128)}, f32[4,144,256]{2,1,0:T(8,128)}) custom-call(s32[5,16]{1,0:T(8,128)} %stack.67.refs_0_, f32[16,2,72,128]{3,2,1,0:T(8,128)} %bitcast.118, f32[4,144,256]{2,1,0:T(8,128)} %get-tuple-element.45.refs_2_, f32[4,144,256]{2,1,0:T(8,128)} %get-tuple-element.46.refs_3_), custom_call_target="tpu_custom_call" | custom-call | flops 1000000 | bytes 100000000 | tf_op jit(solution)/shard_map/halo/pallas_call | solution.py:615
  230.6 29.4 %last_step.1 = (f32[8,1152,256]{2,1,0:T(8,128)}, f32[16,48,256]{2,1,0:T(8,128)}) custom-call(s32[11,8]{1,0:T(8,128)} %stack.56.tab, f32[8,1152,256]{2,1,0:T(8,128)} %get-tuple-element.43.c_ref, f32[8,224,256]{2,1,0:T(8,128)} %bitcast.113, f32[8,2,2,72,128]{4,3,2,1,0:T(8,128)} %bitcast.116, f32[4,144,256]{2,1,0:T(8,128)} %get-tuple-element.48.west, ...), custom_call_target="tpu_custom_call" | custom-call | flops 100000000 | bytes 25000000 | tf_op jit(solution)/shard_map/last_step/pallas_call | solution.py:352
  260.0 22.3 %all_to_all.5.got = f32[16,48,256]{2,1,0:T(8,128)} all-to-all(f32[16,48,256]{2,1,0:T(8,128)} %get-tuple-element.51), channel_id=1, replica_groups=mesh['lat'=8,'lon'=16] {'lon'}, dimensions={0} | all-to-all | bytes 1572864 | tf_op jit(solution)/shard_map/all_to_all | solution.py:732
  282.3 5.2 %heat.1 = bf16[48,48,384]{2,1,0:T(8,128)(2,1)} custom-call(s32[11,8]{1,0:T(8,128)} %stack.56.tab, f32[16,48,256]{2,1,0:T(8,128)} %all_to_all.5.got, f32[16,128]{1,0:T(8,128)} %copy-done.2, f32[48,384]{1,0:T(8,128)} %light.1), custom_call_target="tpu_custom_call" | custom-call | flops 1000000000 | bytes 3000000 | tf_op jit(solution)/shard_map/heat/pallas_call | solution.py:658
  (74 shorter events, 11.9 us)
Async XLA Ops:
  1.3 31.7 %copy-start.2 = (f32[16,128]{1,0:T(8,128)}, f32[16,128]{1,0:T(8,128)S(1)}, u32[]{:S(2)}) copy-start(f32[16,128]{1,0:T(8,128)S(1)} %convert_element_type.63.wet) | copy-start | bytes 24580
  1.5 22.2 %collective-permute-start.1 = (f32[16]{0:T(128)S(1)}, f32[16]{0:T(128)S(1)}, u32[]{:S(2)}, u32[]{:S(2)}) collective-permute-start(f32[16]{0:T(128)S(1)} %get-tuple-element.52), channel_id=1, source_target_pairs={{0,15},{1,0},{2,1},{3,2},{4,3},{5,4},{6,5},{7,6},{8,7},{9,8},{10,9... | collective-permute-start | bytes 200 | tf_op jit(solution)/shard_map/ppermute | solution.py:728
  8.1 15.8 %collective-permute-start = (f32[16]{0:T(128)S(1)}, f32[16]{0:T(128)S(1)}, u32[]{:S(2)}, u32[]{:S(2)}) collective-permute-start(f32[16]{0:T(128)S(1)} %get-tuple-element.53), channel_id=1, source_target_pairs={{0,1},{1,2},{2,3},{3,4},{4,5},{5,6},{6,7},{7,8},{8,9},{9,10},{10,1... | collective-permute-start | bytes 200 | tf_op jit(solution)/shard_map/ppermute | solution.py:728
  8.7 15.2 %collective-permute-start.3 = (f32[256]{0:T(256)S(1)}, f32[256]{0:T(256)S(1)}, u32[]{:S(2)}, u32[]{:S(2)}) collective-permute-start(f32[256]{0:T(256)S(1)} %get-tuple-element.94), channel_id=1, source_target_pairs={{0,112},{16,0},{32,16},{48,32},{64,48},{80,64},{96,80},{112,96},{1... | collective-permute-start | bytes 3080 | tf_op jit(solution)/shard_map/ppermute | solution.py:728
  8.7 15.2 %collective-permute-start.2 = (f32[256]{0:T(256)S(1)}, f32[256]{0:T(256)S(1)}, u32[]{:S(2)}, u32[]{:S(2)}) collective-permute-start(f32[256]{0:T(256)S(1)} %get-tuple-element.95), channel_id=1, source_target_pairs={{0,16},{16,32},{32,48},{48,64},{64,80},{80,96},{96,112},{112,0},{1... | collective-permute-start | bytes 3080 | tf_op jit(solution)/shard_map/ppermute | solution.py:728
  33.7 17.9 %collective-permute-start.5 = (f32[48,128]{1,0:T(8,128)S(1)}, f32[48,128]{1,0:T(8,128)S(1)}, u32[]{:S(2)}, u32[]{:S(2)}) collective-permute-start(f32[48,128]{1,0:T(8,128)S(1)} %slice_bitcast_fusion), channel_id=1, source_target_pairs={{0,16},{16,32},{32,48},{48,64},{64,80},{80,96},{96,112},{112,0},{1... | collective-permute-start | bytes 73736 | tf_op jit(solution)/shard_map/ppermute | solution.py:728
  34.9 16.8 %collective-permute-start.4 = (f32[48,128]{1,0:T(8,128)}, f32[48,128]{1,0:T(8,128)S(1)}, u32[]{:S(2)}, u32[]{:S(2)}) collective-permute-start(f32[48,128]{1,0:T(8,128)} %get-tuple-element.38), channel_id=1, source_target_pairs={{0,1},{1,2},{2,3},{3,4},{4,5},{5,6},{6,7},{7,8},{8,9},{9,10},{10,1... | collective-permute-start | bytes 73736 | tf_op jit(solution)/shard_map/ppermute | solution.py:728
  45.5 94.1 %collective-permute-start.6 = (f32[4,144,256]{2,1,0:T(8,128)}, f32[4,144,256]{2,1,0:T(8,128)S(1)}, u32[]{:S(2)}, u32[]{:S(2)}) collective-permute-start(f32[4,144,256]{2,1,0:T(8,128)} %get-tuple-element.41), channel_id=1, source_target_pairs={{0,1},{1,2},{2,3},{3,4},{4,5},{5,6},{6,7},{7,8},{8,9},{9,10},{10,1... | collective-permute-start | bytes 1769480 | tf_op jit(solution)/shard_map/ppermute | solution.py:728
  45.5 94.1 %collective-permute-start.7 = (f32[4,144,256]{2,1,0:T(8,128)}, f32[4,144,256]{2,1,0:T(8,128)S(1)}, u32[]{:S(2)}, u32[]{:S(2)}) collective-permute-start(f32[4,144,256]{2,1,0:T(8,128)} %get-tuple-element.42), channel_id=1, source_target_pairs={{0,15},{1,0},{2,1},{3,2},{4,3},{5,4},{6,5},{7,6},{8,7},{9,8},{10,9... | collective-permute-start | bytes 1769480 | tf_op jit(solution)/shard_map/ppermute | solution.py:728
  51.7 0.6 copy-start.3
  52.3 0.6 copy-start.4
  139.6 0.8 copy-start
  139.6 1.0 copy-start.1
